TPU v7x, 32 devices: a whole 2x2x4 slice. The times are simulated.
32 devices in a mesh: seq: 8 (over y, x, core), head: 4 (over z).
Axes of the slice: x: 2, y: 2, z: 4, core: 2. Of those that a mesh axis runs over, the one named last changes fastest.
Arguments:
- stream: bfloat16 [2048, 768], P('seq'), may hold values from -6 to 6
- seq_flags: int32 [2048], P('seq'), may hold values from 0 to 1, as said below
- norm_gain: float32 [2, 768], replicated, may hold values from 0.5 to 1.5
- in_zx: bfloat16 [2, 2, 768, 1536], P(None, None, None, 'head'), may hold values from -0.21875 to 0.21875
- in_bc: bfloat16 [2, 768, 256], replicated, may hold values from -0.21875 to 0.21875
- in_dt: bfloat16 [2, 768, 24], P(None, None, 'head'), may hold values from -0.109375 to 0.109375
- dt_bias: float32 [2, 24], P(None, 'head'), may hold values from -4 to -1
- a_log: float32 [2, 24], P(None, 'head'), may hold values from -7 to 1
- skip_d: float32 [2, 24], P(None, 'head'), may hold values from 0.5 to 1.5
- conv_x: float32 [2, 4, 1536], P(None, None, 'head'), may hold values from -3 to 3
- conv_x_bias: float32 [2, 1536], P(None, 'head'), may hold values from -0.5 to 0.5
- conv_bc: float32 [2, 4, 256], replicated, may hold values from -3 to 3
- conv_bc_bias: float32 [2, 256], replicated, may hold values from -0.5 to 0.5
- gate_gain: float32 [2, 1536], P(None, 'head'), may hold values from 0.5 to 1.5
- out_proj: bfloat16 [2, 1536, 768], P(None, 'head'), may hold values from -0.15625 to 0.15625
- cotangent: bfloat16 [2048, 768], P('seq'), may hold values from -6 to 6
Outputs:
- output: float32 [2048, 768], P('seq')
- grad_stream: float32 [2048, 768], P('seq')
- grad_norm_gain: float32 [2, 768], replicated
- grad_in_zx: float32 [2, 2, 768, 1536], P(None, None, None, 'head')
- grad_in_bc: float32 [2, 768, 256], replicated
- grad_in_dt: float32 [2, 768, 24], P(None, None, 'head')
- grad_dt_bias: float32 [2, 24], P(None, 'head')
- grad_a_log: float32 [2, 24], P(None, 'head')
- grad_skip_d: float32 [2, 24], P(None, 'head')
- grad_conv_x: float32 [2, 4, 1536], P(None, None, 'head')
- grad_conv_x_bias: float32 [2, 1536], P(None, 'head')
- grad_conv_bc: float32 [2, 4, 256], replicated
- grad_conv_bc_bias: float32 [2, 256], replicated
- grad_gate_gain: float32 [2, 1536], P(None, 'head')
- grad_out_proj: float32 [2, 1536, 768], P(None, 'head')
Inputs may be any that keep to these rules, and one draw needn't show every extreme that they name: seq_flags is 1 at position 0, and every other 1 stands at a position that is a multiple of 8.
All inputs are finite; a program needn't handle non-finite values.
Results may differ from a plain program's by a relative error of at most 0.04.
Values may be sent and summed in bfloat16 or wider, within the bound.
No kernel may reach another device: no remote copies, remote signals or barrier semaphores. Data moves between devices by JAX's collectives and lax.ppermute only.
A program may use at most 128 MiB of HBM per device.

v0:
```python
import jax
import jax.numpy as jnp
from jax import lax
from jax.sharding import PartitionSpec as P

P_SIZE = 64
N = 128
LAYERS = 2
DI = 1536


EPS = 1e-05
PRECISE = lax.Precision.HIGHEST


def passed_along(array, axis, by):
    devices = lax.axis_size(axis)
    pairs = [(i, i + by) for i in range(devices) if 0 <= i + by < devices]
    return lax.ppermute(array, axis, pairs)


def prefix(part, axis, combine, identity):
    place = lax.axis_index(axis)
    gathered = jax.tree.map(lambda a: lax.all_gather(a, axis), part)
    state = jax.tree.map(lambda a, e: jnp.zeros_like(a) + jnp.asarray(e, a.dtype), part, identity)

    def one(turn, state):
        return combine(
            state, jax.tree.map(lambda a: lax.dynamic_index_in_dim(a, turn, 0, False), gathered)
        )

    return lax.fori_loop(0, place, one, state)


def carried_in(array, axis, combine, identity):
    devices, position = (lax.axis_size(axis), lax.axis_index(axis))
    everything = jax.tree.map(
        lambda part, kind: lax.all_gather(part.astype(kind), axis),
        array,
        jax.tree.map(lambda a: jnp.bfloat16 if a.dtype == jnp.float32 else a.dtype, array),
    )
    start = jax.tree.map(
        lambda part, zero: jnp.broadcast_to(jnp.asarray(zero, part.dtype), part.shape),
        array,
        identity,
    )

    def turn(k, before):
        at = devices - 1 - k
        reached = at > position
        new = combine(
            before, jax.tree.map(lambda part, own: part[at].astype(own.dtype), everything, array)
        )
        return jax.tree.map(lambda a, b: jnp.where(reached, a, b), new, before)

    return lax.fori_loop(0, devices, turn, start)


def contract_rows(left, right):
    return lax.dot_general(
        left, right, (((0,), (0,)), ((), ())), preferred_element_type=jnp.float32
    )


def outer_t(left, right):
    return lax.dot_general(
        left, right, (((1,), (1,)), ((), ())), preferred_element_type=jnp.float32
    )


def norm_rows(residual, gain_row):
    inv_rms = lax.rsqrt(jnp.mean(residual * residual, axis=1, keepdims=True) + EPS)
    return residual * inv_rms * gain_row[None, :]


def conv_causal(extended, weights, conv_bias, starts_ext):
    conv_taps = weights.shape[0]
    length = extended.shape[0] - conv_taps + 1
    running = jnp.cumsum(starts_ext)
    result = jnp.zeros((length, extended.shape[1]), extended.dtype) + conv_bias[None, :]
    for offset in range(conv_taps):
        first_row = conv_taps - 1 - offset
        source = extended[first_row : first_row + length]
        counts = (
            running[conv_taps - 1 : conv_taps - 1 + length]
            - running[first_row : first_row + length]
        )
        validity = jnp.where(counts == 0, 1.0, 0.0).astype(extended.dtype)
        result = result + weights[first_row][None, :] * source * validity[:, None]
    return result


def ssd_group(carry_state, values, keys_in, queries, step_sizes, rates, starts):
    decay_log = step_sizes * rates[None, :]
    cumulative = jnp.cumsum(decay_log, axis=0)
    segment = jnp.cumsum(starts)
    length = starts.shape[0]
    rows_idx = lax.broadcasted_iota(jnp.int32, (length, length), 0)
    cols_idx = lax.broadcasted_iota(jnp.int32, (length, length), 1)
    allowed = (rows_idx >= cols_idx) & (segment[:, None] == segment[None, :])
    spread = cumulative.T[:, :, None] - cumulative.T[:, None, :]
    decay_mat = jnp.where(allowed[None], jnp.exp(jnp.where(allowed[None], spread, 0.0)), 0.0)
    scores = jnp.dot(queries, keys_in.T, precision=PRECISE)
    mixing = decay_mat * scores[None] * step_sizes.T[:, None, :]
    inside = jnp.einsum("hts,shp->thp", mixing, values, precision=PRECISE)
    opening = jnp.exp(cumulative) * jnp.where(segment == 0, 1.0, 0.0)[:, None]
    carried = (
        jnp.einsum("tn,hnp->thp", queries, carry_state, precision=PRECISE) * opening[:, :, None]
    )
    closing = (
        jnp.exp(cumulative[-1][None, :] - cumulative)
        * jnp.where(segment == segment[-1], 1.0, 0.0)[:, None]
        * step_sizes
    )
    kept_share = jnp.exp(cumulative[-1]) * jnp.where(segment[-1] == 0, 1.0, 0.0)
    new_state = carry_state * kept_share[:, None, None] + jnp.einsum(
        "sn,shp->hnp", keys_in, values * closing[:, :, None], precision=PRECISE
    )
    return (inside + carried, new_state)


def local_ssd(carry_state, values, keys_in, queries, step_sizes, rates, starts):
    result, carry_state = ssd_group(
        carry_state, values, keys_in, queries, step_sizes, rates, starts
    )
    results = [result]
    return (jnp.concatenate(results, axis=0), carry_state)


def chain_combine(earlier, later):
    return (earlier[0] * later[0], later[0][:, None, None] * earlier[1] + later[1])


def layer_forward(residual, starts, params):
    (
        norm_gain,
        in_zx,
        in_bc,
        in_dt,
        dt_bias,
        a_log,
        skip_d,
        conv_x,
        conv_x_bias,
        conv_bc,
        conv_bc_bias,
        gate_gain,
        out_proj,
    ) = params
    tokens = residual.shape[0]
    local_width = conv_x.shape[1]
    head_count = local_width // P_SIZE
    conv_taps = conv_x.shape[0]
    normed = norm_rows(residual, norm_gain).astype(jnp.bfloat16)
    gate_in = jnp.dot(normed, in_zx[0], preferred_element_type=jnp.float32)
    before = jnp.concatenate(
        [
            jnp.dot(normed, in_zx[1], preferred_element_type=jnp.float32).astype(jnp.bfloat16),
            jnp.dot(normed, in_bc, preferred_element_type=jnp.float32).astype(jnp.bfloat16),
        ],
        axis=1,
    )
    dt_raw = jnp.dot(normed, in_dt, preferred_element_type=jnp.float32)
    rim_rows = passed_along(before[tokens - conv_taps + 1 :], "seq", 1)
    extended = jnp.concatenate([rim_rows, before], axis=0).astype(jnp.float32)
    starts_ext = jnp.concatenate([jnp.zeros((conv_taps - 1,), jnp.float32), starts])
    weights = jnp.concatenate([conv_x, conv_bc], axis=1)
    conv_bias = jnp.concatenate([conv_x_bias, conv_bc_bias])
    activated = jax.nn.silu(conv_causal(extended, weights, conv_bias, starts_ext)).astype(
        jnp.bfloat16
    )
    act_wide = activated.astype(jnp.float32)
    values = act_wide[:, :local_width].reshape(tokens, head_count, P_SIZE)
    keys_in = act_wide[:, local_width : local_width + N]
    queries = act_wide[:, local_width + N :]
    step_sizes = jax.nn.softplus(dt_raw + dt_bias[None, :])
    rates = -jnp.exp(a_log)
    zero_state = jnp.zeros((head_count, N, P_SIZE), jnp.float32)
    partial_out, local_state = local_ssd(
        zero_state, values, keys_in, queries, step_sizes, rates, starts
    )
    cumulative = jnp.cumsum(step_sizes * rates[None, :], axis=0)
    segment = jnp.cumsum(starts)
    opening = jnp.exp(cumulative) * jnp.where(segment == 0, 1.0, 0.0)[:, None]
    through = jnp.exp(cumulative[-1]) * jnp.where(segment[-1] == 0, 1.0, 0.0)
    _, state_in = prefix(
        (through, local_state),
        "seq",
        chain_combine,
        (jnp.ones_like(through), jnp.zeros_like(local_state)),
    )
    mixed_out = (
        partial_out
        + jnp.einsum("tn,hnp->thp", queries, state_in, precision=PRECISE) * opening[:, :, None]
    )
    mixed_out = mixed_out + skip_d[None, :, None] * values
    gate_act = jax.nn.silu(gate_in)
    gated_out = mixed_out.reshape(tokens, local_width) * gate_act
    square_sum = lax.psum(jnp.sum(gated_out * gated_out, axis=1), "head")
    inv_rms = lax.rsqrt(square_sum[:, None] / DI + EPS)
    outgoing = (gated_out * inv_rms * gate_gain[None, :]).astype(jnp.bfloat16)
    share_rows = tokens // lax.axis_size("head")
    offset_row = lax.axis_index("head") * share_rows
    mixer_part = lax.psum_scatter(
        jnp.dot(outgoing, out_proj, preferred_element_type=jnp.float32),
        "head",
        scatter_dimension=0,
        tiled=True,
    )
    resid_share = lax.dynamic_slice_in_dim(residual, offset_row, share_rows, 0)
    next_stream = lax.all_gather(resid_share + mixer_part, "head", axis=0, tiled=True)
    stored = (
        normed,
        gate_in,
        dt_raw,
        extended,
        starts_ext,
        weights,
        conv_bias,
        values,
        keys_in,
        queries,
        step_sizes,
        rates,
        state_in,
        through,
        opening,
        mixed_out,
        gated_out,
        inv_rms,
        outgoing,
        share_rows,
        offset_row,
    )
    return (next_stream, stored)


def layer_backward(residual, starts, params, stored, grad_next):
    (
        norm_gain,
        in_zx,
        in_bc,
        in_dt,
        dt_bias,
        a_log,
        skip_d,
        conv_x,
        conv_x_bias,
        conv_bc,
        conv_bc_bias,
        gate_gain,
        out_proj,
    ) = params
    (
        normed,
        gate_in,
        dt_raw,
        extended,
        starts_ext,
        weights,
        conv_bias,
        values,
        keys_in,
        queries,
        step_sizes,
        rates,
        state_in,
        through,
        opening,
        mixed_out,
        gated_out,
        inv_rms,
        outgoing,
        share_rows,
        offset_row,
    ) = stored
    tokens = residual.shape[0]
    local_width = conv_x.shape[1]
    head_count = local_width // P_SIZE
    conv_taps = conv_x.shape[0]
    low_grad = grad_next.astype(jnp.bfloat16)
    grad_out_proj = contract_rows(outgoing, low_grad)
    grad_outgoing = outer_t(low_grad, out_proj)
    cross_sum = lax.psum(jnp.sum(grad_outgoing * gate_gain[None, :] * gated_out, axis=1), "head")
    g_gate_gain = jnp.sum(grad_outgoing * gated_out * inv_rms, axis=0)
    g_gated = (
        inv_rms * gate_gain[None, :] * grad_outgoing
        - gated_out * inv_rms**3 * cross_sum[:, None] / DI
    )
    gate_sig = jax.nn.sigmoid(gate_in)
    gate_act = gate_in * gate_sig
    g_mixed = (g_gated * gate_act).reshape(tokens, head_count, P_SIZE)
    g_gate = (
        g_gated
        * mixed_out.reshape(tokens, local_width)
        * gate_sig
        * (1.0 + gate_in * (1.0 - gate_sig))
    )
    g_skip = jnp.sum(g_mixed * values, axis=(0, 2))
    local_grad = jnp.einsum("th,tn,thp->hnp", opening, queries, g_mixed, precision=PRECISE)
    _, state_grad = carried_in(
        (through, local_grad),
        "seq",
        chain_combine,
        (jnp.ones_like(through), jnp.zeros_like(local_grad)),
    )

    def ssd_fn(vals_in, keys_val, query_val, sizes_val, rates_val):
        return local_ssd(state_in, vals_in, keys_val, query_val, sizes_val, rates_val, starts)

    _, pull_ssd = jax.vjp(ssd_fn, values, keys_in, queries, step_sizes, rates)
    g_values, g_keys, g_queries, g_steps, g_rates = pull_ssd((g_mixed, state_grad))
    g_values = g_values + skip_d[None, :, None] * g_mixed
    g_a_log = g_rates * rates
    g_raw = g_steps * jax.nn.sigmoid(dt_raw + dt_bias[None, :])
    g_dt_bias = jnp.sum(g_raw, axis=0)
    g_keys, g_queries = (
        lax.psum(g_keys.astype(jnp.bfloat16), "head").astype(jnp.float32),
        lax.psum(g_queries.astype(jnp.bfloat16), "head").astype(jnp.float32),
    )
    g_act = jnp.concatenate([g_values.reshape(tokens, local_width), g_keys, g_queries], axis=1)

    def conv_fn(ext_val, wts_val, bias_val):
        return jax.nn.silu(conv_causal(ext_val, wts_val, bias_val, starts_ext))

    _, pull_conv = jax.vjp(conv_fn, extended, weights, conv_bias)
    g_ext, g_weights, g_bias = pull_conv(g_act)
    returned = passed_along(g_ext[: conv_taps - 1], "seq", -1)
    channels = g_ext.shape[1]
    g_before = g_ext[conv_taps - 1 :] + jnp.concatenate(
        [jnp.zeros((tokens - conv_taps + 1, channels), jnp.float32), returned], axis=0
    )
    low_gate = g_gate.astype(jnp.bfloat16)
    low_conv = g_before.astype(jnp.bfloat16)
    low_raw = g_raw.astype(jnp.bfloat16)
    low_x = low_conv[:, :local_width]
    low_bc = low_conv[:, local_width:]
    grad_in_zx = jnp.stack([contract_rows(normed, low_gate), contract_rows(normed, low_x)])
    grad_in_bc = contract_rows(normed, low_bc)
    grad_in_dt = contract_rows(normed, low_raw)
    normed_part = lax.psum_scatter(
        (outer_t(low_gate, in_zx[0]) + outer_t(low_x, in_zx[1]) + outer_t(low_raw, in_dt)).astype(
            jnp.bfloat16
        ),
        "head",
        scatter_dimension=0,
        tiled=True,
    ).astype(jnp.float32)
    normed_part = normed_part + outer_t(
        lax.dynamic_slice_in_dim(low_bc, offset_row, share_rows, 0), in_bc
    )
    g_normed = lax.all_gather(normed_part.astype(jnp.bfloat16), "head", axis=0, tiled=True).astype(
        normed_part.dtype
    )
    _, pull_norm = jax.vjp(norm_rows, residual, norm_gain)
    g_resid, g_norm_gain = pull_norm(g_normed)
    weight_grads = (
        g_norm_gain,
        grad_in_zx,
        grad_in_bc,
        grad_in_dt,
        g_dt_bias,
        g_a_log,
        g_skip,
        g_weights[:, :local_width],
        g_bias[:local_width],
        g_weights[:, local_width:],
        g_bias[local_width:],
        g_gate_gain,
        grad_out_proj,
    )
    return (grad_next + g_resid, weight_grads)


def per_device(
    stream,
    seq_flags,
    norm_gain,
    in_zx,
    in_bc,
    in_dt,
    dt_bias,
    a_log,
    skip_d,
    conv_x,
    conv_x_bias,
    conv_bc,
    conv_bc_bias,
    gate_gain,
    out_proj,
    cotangent,
):
    starts = seq_flags.astype(jnp.float32)
    params_all = (
        norm_gain,
        in_zx,
        in_bc,
        in_dt,
        dt_bias,
        a_log,
        skip_d,
        conv_x,
        conv_x_bias,
        conv_bc,
        conv_bc_bias,
        gate_gain,
        out_proj,
    )
    residual = stream.astype(jnp.float32)
    inputs_kept = []
    stores = []
    for depth in range(LAYERS):
        params = tuple((member[depth] for member in params_all))
        inputs_kept.append(residual)
        residual, stored = layer_forward(residual, starts, params)
        stores.append(stored)
    gradient = cotangent.astype(jnp.float32)
    per_layer = [None] * LAYERS
    for depth in reversed(range(LAYERS)):
        params = tuple((member[depth] for member in params_all))
        gradient, weight_grads = layer_backward(
            inputs_kept[depth], starts, params, stores[depth], gradient
        )
        weight_grads = (
            lax.psum(weight_grads[0].astype(jnp.bfloat16), "seq").astype(jnp.float32),
            lax.psum(weight_grads[1].astype(jnp.bfloat16), "seq").astype(jnp.float32),
            lax.psum(weight_grads[2].astype(jnp.bfloat16), "seq").astype(jnp.float32),
            lax.psum(weight_grads[3].astype(jnp.bfloat16), "seq").astype(jnp.float32),
            lax.psum(weight_grads[4].astype(jnp.bfloat16), "seq").astype(jnp.float32),
            lax.psum(weight_grads[5].astype(jnp.bfloat16), "seq").astype(jnp.float32),
            lax.psum(weight_grads[6].astype(jnp.bfloat16), "seq").astype(jnp.float32),
            lax.psum(weight_grads[7].astype(jnp.bfloat16), "seq").astype(jnp.float32),
            lax.psum(weight_grads[8].astype(jnp.bfloat16), "seq").astype(jnp.float32),
            lax.psum(weight_grads[9].astype(jnp.bfloat16), "seq").astype(jnp.float32),
            lax.psum(weight_grads[10].astype(jnp.bfloat16), "seq").astype(jnp.float32),
            lax.psum(weight_grads[11].astype(jnp.bfloat16), "seq").astype(jnp.float32),
            lax.psum(weight_grads[12].astype(jnp.bfloat16), "seq").astype(jnp.float32),
        )
        per_layer[depth] = weight_grads
    stacked = [
        jnp.stack([per_layer[depth][number] for depth in range(LAYERS)]) for number in range(13)
    ]
    return (
        residual,
        gradient,
        stacked[0],
        stacked[1],
        stacked[2],
        stacked[3],
        stacked[4],
        stacked[5],
        stacked[6],
        stacked[7],
        stacked[8],
        stacked[9],
        stacked[10],
        stacked[11],
        stacked[12],
    )


def solution(mesh):
    placed = (
        P("seq", None),
        P("seq"),
        P(),
        P(None, None, None, "head"),
        P(),
        P(None, None, "head"),
        P(None, "head"),
        P(None, "head"),
        P(None, "head"),
        P(None, None, "head"),
        P(None, "head"),
        P(),
        P(),
        P(None, "head"),
        P(None, "head", None),
        P("seq", None),
    )
    return jax.shard_map(
        per_device,
        mesh=mesh,
        in_specs=placed,
        out_specs=(
            P("seq", None),
            P("seq", None),
            P(),
            P(None, None, None, "head"),
            P(),
            P(None, None, "head"),
            P(None, "head"),
            P(None, "head"),
            P(None, "head"),
            P(None, None, "head"),
            P(None, "head"),
            P(),
            P(),
            P(None, "head"),
            P(None, "head", None),
        ),
        check_vma=False,
    )
```

profile of v0, /device:TPU:0, one launch (start us, length us, event | category | flops | bytes accessed | tf_op | source)
XLA Modules:
  0.0 636.9 jit_solution(3372900655773263176)
XLA Ops:
  28.4 9.8 %all-gather.4 = f32[8,1,6]{2,1,0:T(1,128)S(1)} all-gather(f32[1,1,6]{2,1,0:T(1,128)S(1)} %bitcast.619), channel_id=1, replica_groups=mesh['seq'=8,'head'=4] {'seq'}, dimensions={0}, use_global_device_ids=true | all-gather | bytes 216 | tf_op jit(solution)/shard_map/all_gather | solution.py:24
  41.5 15.1 %all-gather.11.cloned.1.call-done = f32[48,128,64]{1,2,0:T(8,128)} async-done(((f32[6,128,64]{1,2,0:T(8,128)}), f32[48,128,64]{1,2,0:T(8,128)}) %all-gather.11.cloned.1.call-update) | async-done | bytes 1572880 | tf_op jit(solution)/shard_map/all_gather | solution.py:24
  57.4 3.2 fusion.67
  64.3 11.7 %psum.238 = f32[256]{0:T(256)S(1)} all-reduce(f32[256]{0:T(256)S(1)} %get-tuple-element.685), channel_id=1, replica_groups=mesh['seq'=8,'head'=4] {'head'}, use_global_device_ids=true, to_apply=%region_10.11 | all-reduce | flops 256 | bytes 2048 | tf_op jit(solution)/shard_map/psum | solution.py:199
  80.1 27.1 %reduce-scatter.5.cloned.1.call-done = f32[64,768]{1,0:T(8,128)} async-done(((f32[256,768]{1,0:T(8,128)}), f32[64,768]{1,0:T(8,128)}) %reduce-scatter.5.cloned.1.call-update) | async-done | bytes 196624 | tf_op jit(solution)/shard_map/reduce_scatter | solution.py:204
  108.3 18.0 %all_gather.55 = f32[256,768]{1,0:T(8,128)S(1)} all-gather(f32[64,768]{1,0:T(8,128)S(1)} %dynamic-slice_add_fusion.1), channel_id=1, replica_groups=mesh['seq'=8,'head'=4] {'head'}, dimensions={0}, use_global_device_ids=true | all-gather | bytes 983040 | tf_op jit(solution)/shard_map/all_gather | solution.py:211
  140.4 9.4 %all-gather.6 = bf16[8,1,6]{2,1,0:T(2,128)(2,1)S(1)} all-gather(bf16[1,1,6]{2,1,0:T(2,128)(2,1)S(1)} %bitcast.617), channel_id=1, replica_groups=mesh['seq'=8,'head'=4] {'seq'}, dimensions={0}, use_global_device_ids=true | all-gather | bytes 108 | tf_op jit(solution)/shard_map/all_gather | solution.py:38
  149.7 9.5 %all-gather.5 = f32[8,1,6]{2,1,0:T(1,128)} all-gather(f32[1,1,6]{2,1,0:T(1,128)} %bitcast.620), channel_id=1, replica_groups=mesh['seq'=8,'head'=4] {'seq'}, dimensions={0}, use_global_device_ids=true | all-gather | bytes 216 | tf_op jit(solution)/shard_map/all_gather | solution.py:24
  165.6 11.1 %while.57 = (s32[]{:T(128)}, f32[6,128,64]{2,1,0:T(8,128)S(1)}, s32[]{:T(128)}, f32[8,6]{1,0:T(8,128)}, f32[8,6,128,64]{2,3,1,0:T(8,128)}, /*index=5*/s32[]{:T(128)}, s32[]{:T(128)}, s32[]{:T(128)}) while((s32[]{:T(128)}, f32[6,128,64]{2,1,0:T(8,128)S(1)}, s32[]{:T(128)}, f32[8,6]{1,0:T(8,128)}, f32[8,6,128,64]{2,3,1,0:T(8,128)}, ...), condition=%wide.region_16.17_spmd, body=%wide.region_15.16_spmd.sunk | while | flops 98309 | bytes 1376463 | solution.py:32
  178.0 3.7 fusion.64
  186.0 11.8 %psum.239 = f32[256]{0:T(256)S(1)} all-reduce(f32[256]{0:T(256)S(1)} %get-tuple-element.681), channel_id=1, replica_groups=mesh['seq'=8,'head'=4] {'head'}, use_global_device_ids=true, to_apply=%region_18.19 | all-reduce | flops 256 | bytes 2048 | tf_op jit(solution)/shard_map/psum | solution.py:199
  197.8 3.0 multiply_reduce_fusion.14
  200.8 8.3 %psum.240 = f32[256]{0:T(256)S(1)} all-reduce(f32[256]{0:T(256)S(1)} %get-tuple-element.568), channel_id=1, replica_groups=mesh['seq'=8,'head'=4] {'head'}, use_global_device_ids=true, to_apply=%region_21.22 | all-reduce | flops 256 | bytes 2048 | tf_op jit(solution)/shard_map/psum | solution.py:284
  216.4 22.3 %all-gather.2 = bf16[48,128,64]{1,2,0:T(8,128)(2,1)} all-gather(bf16[6,128,64]{1,2,0:T(8,128)(2,1)S(1)} %fusion.78), channel_id=4, replica_groups=mesh['seq'=8,'head'=4] {'seq'}, dimensions={0}, use_global_device_ids=true | all-gather | bytes 884736 | tf_op jit(solution)/shard_map/all_gather | solution.py:38
  238.7 15.4 %while.58 = (s32[]{:T(128)}, f32[6,128,64]{2,1,0:T(8,128)S(1)}, s32[]{:T(128)}, bf16[8,6]{1,0:T(8,128)(2,1)}, bf16[8,6,128,64]{2,3,1,0:T(8,128)(2,1)}, /*index=5*/s32[]{:T(128)}, s32[]{:T(128)}, s32[]{:T(128)}, s32[]{:T(128)}) while((s32[]{:T(128)}, f32[6,128,64]{2,1,0:T(8,128)S(1)}, s32[]{:T(128)}, bf16[8,6]{1,0:T(8,128)(2,1)}, ...), condition=%wide.region_23.24_spmd.clone, body=%wide.region_22.23_spmd.clone.sunk | while | flops 245774 | bytes 884971 | solution.py:56
  272.5 8.8 %reduce-window.56 = f32[6,2,128]{2,1,0:T(2,128)} reduce-window(f32[6,2,128]{2,1,0:T(2,128)} %reshape.525, f32[]{:T(128)} %constant.189.clone.1), window={size=1x1x128 pad=0_0x0_0x0_127}, to_apply=%region_34.35 | reduce-window | flops 195072 | bytes 12292 | tf_op jit(solution)/shard_map/reduce-window.8
  298.9 32.6 %all-reduce.36.cloned.1.call-done = (bf16[256,128]{1,0:T(8,128)(2,1)}, bf16[256,128]{1,0:T(8,128)(2,1)}) async-done(((bf16[256,128]{1,0:T(8,128)(2,1)}, bf16[256,128]{1,0:T(8,128)(2,1)}), (bf16[256,128]{1,0:T(8,128)(2,1)}, bf16[256,128]{1,0:T(8,128)(2,1)})) %all-reduce.36.cloned.1.call-update) | async-done | bytes 131088 | tf_op jit(solution)/shard_map/psum | solution.py:319
  341.4 10.0 %all-gather.7 = bf16[8,1,6]{2,1,0:T(2,128)(2,1)} all-gather(bf16[1,1,6]{2,1,0:T(2,128)(2,1)S(1)} %bitcast.618), channel_id=1, replica_groups=mesh['seq'=8,'head'=4] {'seq'}, dimensions={0}, use_global_device_ids=true | all-gather | bytes 108 | tf_op jit(solution)/shard_map/all_gather | solution.py:38
  363.7 15.1 %all_gather.63 = bf16[256,768]{1,0:T(8,128)(2,1)S(1)} all-gather(bf16[64,768]{1,0:T(8,128)(2,1)S(1)} %fusion.72), channel_id=1, replica_groups=mesh['seq'=8,'head'=4] {'head'}, dimensions={0}, use_global_device_ids=true | all-gather | bytes 491520 | tf_op jit(solution)/shard_map/all_gather | solution.py:352
  382.6 8.3 %psum.243 = f32[256]{0:T(256)S(1)} all-reduce(f32[256]{0:T(256)S(1)} %get-tuple-element.566), channel_id=1, replica_groups=mesh['seq'=8,'head'=4] {'head'}, use_global_device_ids=true, to_apply=%region_39.40 | all-reduce | flops 256 | bytes 2048 | tf_op jit(solution)/shard_map/psum | solution.py:284
  390.9 3.1 multiply_reduce_fusion.17
  397.3 3.1 convolution_bitcast_fusion
  400.4 3.7 fusion.89
  404.1 11.7 %all-gather.3 = bf16[48,128,64]{1,2,0:T(8,128)(2,1)} all-gather(bf16[6,128,64]{1,2,0:T(8,128)(2,1)S(1)} %fusion.79), channel_id=5, replica_groups=mesh['seq'=8,'head'=4] {'seq'}, dimensions={0}, use_global_device_ids=true | all-gather | bytes 884736 | tf_op jit(solution)/shard_map/all_gather | solution.py:38
  415.9 27.5 %while.59 = (s32[]{:T(128)}, f32[6,128,64]{2,1,0:T(8,128)S(1)}, s32[]{:T(128)}, bf16[8,6]{1,0:T(8,128)(2,1)}, bf16[8,6,128,64]{2,3,1,0:T(8,128)(2,1)}, /*index=5*/s32[]{:T(128)}, s32[]{:T(128)}, s32[]{:T(128)}, s32[]{:T(128)}) while((s32[]{:T(128)}, f32[6,128,64]{2,1,0:T(8,128)S(1)}, s32[]{:T(128)}, bf16[8,6]{1,0:T(8,128)(2,1)}, ...), condition=%wide.region_41.42_spmd.clone, body=%wide.region_40.41_spmd.clone.sunk | while | flops 245774 | bytes 884971 | solution.py:56
  461.6 7.6 %reduce-window.72 = f32[6,2,128]{2,1,0:T(2,128)S(1)} reduce-window(f32[6,2,128]{2,1,0:T(2,128)S(1)} %reshape.530, f32[]{:T(128)} %constant.189.clone.1), window={size=1x1x128 pad=0_0x0_0x0_127}, to_apply=%region_52.53 | reduce-window | flops 195072 | bytes 12292 | tf_op jit(solution)/shard_map/reduce-window.10
  497.9 11.0 %reduce-scatter.7.cloned.1.call-done = f32[64,768]{1,0:T(8,128)} async-done(((f32[256,768]{1,0:T(8,128)}), f32[64,768]{1,0:T(8,128)}) %reduce-scatter.7.cloned.1.call-update) | async-done | bytes 196624 | tf_op jit(solution)/shard_map/reduce_scatter | solution.py:204
  509.9 22.7 %all_gather.59 = f32[256,768]{1,0:T(8,128)S(1)} all-gather(f32[64,768]{1,0:T(8,128)S(1)} %dynamic-slice_add_fusion), channel_id=1, replica_groups=mesh['seq'=8,'head'=4] {'head'}, dimensions={0}, use_global_device_ids=true | all-gather | bytes 983040 | tf_op jit(solution)/shard_map/all_gather | solution.py:211
  535.5 15.0 %all_gather.67 = bf16[256,768]{1,0:T(8,128)(2,1)S(1)} all-gather(bf16[64,768]{1,0:T(8,128)(2,1)S(1)} %fusion.73), channel_id=1, replica_groups=mesh['seq'=8,'head'=4] {'head'}, dimensions={0}, use_global_device_ids=true | all-gather | bytes 491520 | tf_op jit(solution)/shard_map/all_gather | solution.py:352
  550.9 24.0 %all-reduce.24 = (bf16[1,768]{1,0:T(2,128)(2,1)S(1)}, bf16[1,768]{1,0:T(2,128)(2,1)S(1)}, bf16[1,768,6]{1,2,0:T(8,128)(2,1)S(1)}, bf16[1,768,6]{1,2,0:T(8,128)(2...) all-reduce(bf16[1,768]{1,0:T(2,128)(2,1)S(1)} %stack.207, ...), channel_id=1, replica_groups=mesh['seq'=8,'head'=4] {'seq'}, use_global_device_ids=true, to_apply=%region_59.60 | all-reduce | flops 17956 | bytes 71824 | tf_op jit(solution)/shard_map/psum | solution.py:425
  582.0 39.8 %all-reduce.32.cloned.1.call-done = (bf16[1,2,768,384]{3,2,1,0:T(8,128)(2,1)}, bf16[1,2,768,384]{3,2,1,0:T(8,128)(2,1)}, bf16[1,768,256]{2,1,0:T(8,128)(2,1)}, b...) async-done(((bf16[1,2,768,384]{3,2,1,0:T(8,128)(2,1)}, bf16[1,2,768,384]{3,2,1,0:T(8,128)(2,1)}, ...) | async-done | bytes 4325392 | tf_op jit(solution)/shard_map/psum | solution.py:426
  621.8 4.2 maximum_convert_fusion
  (717 shorter events, 234.7 us)
Async XLA Ops:
  7.2 49.5 %all-gather.11.cloned.1.call-start = ((), (), s32[]{:S(2)}) async-start(), calls=%async_computation.8 | async-start | bytes 1769472 | tf_op jit(solution)/shard_map/all_gather | solution.py:24
  8.0 53.8 %copy-start.103 = (f32[768]{0:T(1024)}, f32[768]{0:T(1024)S(1)}, u32[]{:S(2)}) copy-start(f32[768]{0:T(1024)S(1)} %get-tuple-element.586) | copy-start | bytes 9220
  8.0 118.5 %copy-start.64 = (f32[768]{0:T(1024)}, f32[768]{0:T(1024)S(1)}, u32[]{:S(2)}) copy-start(f32[768]{0:T(1024)S(1)} %get-tuple-element.585) | copy-start | bytes 9220
  12.3 13.2 %collective-permute-start = (bf16[3,640]{1,0:T(4,128)(2,1)S(1)}, bf16[3,640]{1,0:T(4,128)(2,1)S(1)}, u32[]{:S(2)}, u32[]{:S(2)}) collective-permute-start(bf16[3,640]{1,0:T(4,128)(2,1)S(1)} %pad_maximum_fusion.3), channel_id=1, source_target_pairs={{0,4},{4,8},{8,12},{12,16},{16,20},{20,24},{24,28},{1,5},{5,9},{9,... | collective-permute-start | bytes 11528 | tf_op jit(solution)/shard_map/ppermute | solution.py:19
  28.4 78.9 %reduce-scatter.5.cloned.1.call-start = ((), (), s32[]{:S(2)}) async-start(), calls=%async_computation.4 | async-start | bytes 983040 | tf_op jit(solution)/shard_map/reduce_scatter | solution.py:204
  38.8 37.8 %copy-start.78 = (f32[384]{0:T(512)}, f32[384]{0:T(512)S(1)}, u32[]{:S(2)}) copy-start(f32[384]{0:T(512)S(1)} %get-tuple-element.593) | copy-start | bytes 4612
  79.0 86.6 %all-gather.13.cloned.1.call-start = ((), (), s32[]{:S(2)}) async-start(), calls=%async_computation.9 | async-start | bytes 1769472 | tf_op jit(solution)/shard_map/all_gather | solution.py:24
  80.1 56.0 %copy-start.113 = (f32[640]{0:T(1024)}, f32[640]{0:T(1024)S(1)}, u32[]{:S(2)}) copy-start(f32[640]{0:T(1024)S(1)} %get-tuple-element.573) | copy-start | bytes 7684
  80.1 56.0 %copy-start.115 = (f32[640]{0:T(1024)}, f32[640]{0:T(1024)S(1)}, u32[]{:S(2)}) copy-start(f32[640]{0:T(1024)S(1)} %get-tuple-element.574) | copy-start | bytes 7684
  80.1 56.0 %copy-start.117 = (f32[640]{0:T(1024)}, f32[640]{0:T(1024)S(1)}, u32[]{:S(2)}) copy-start(f32[640]{0:T(1024)S(1)} %get-tuple-element.576) | copy-start | bytes 7684
  80.1 56.0 %copy-start.119 = (f32[640]{0:T(1024)}, f32[640]{0:T(1024)S(1)}, u32[]{:S(2)}) copy-start(f32[640]{0:T(1024)S(1)} %get-tuple-element.575) | copy-start | bytes 7684
  129.3 5.8 collective-permute-start.1
  139.5 192.0 %all-reduce.36.cloned.1.call-start = ((), (), s32[]{:S(2)}) async-start(), calls=%async_computation.12 | async-start | bytes 262144 | tf_op jit(solution)/shard_map/psum | solution.py:319
  296.6 36.6 %copy-start.93 = (f32[256]{0:T(256)S(1)}, f32[256]{0:T(256)}, u32[]{:S(2)}) copy-start(f32[256]{0:T(256)} %copy-done.91) | copy-start | bytes 3076
  297.6 64.7 %reduce-scatter.9.cloned.1.call-start = ((), (), s32[]{:S(2)}) async-start(), calls=%async_computation.6 | async-start | bytes 491520 | tf_op jit(solution)/shard_map/reduce_scatter | solution.py:341
  298.9 35.7 %copy-start.101 = (f32[256]{0:T(256)S(1)}, f32[256]{0:T(256)}, u32[]{:S(2)}) copy-start(f32[256]{0:T(256)} %copy-done.99) | copy-start | bytes 3076
  335.5 3.2 collective-permute-start.2
  341.2 143.0 %all-reduce.34.cloned.1.call-start = ((), (), s32[]{:S(2)}) async-start(), calls=%async_computation.11 | async-start | bytes 262144 | tf_op jit(solution)/shard_map/psum | solution.py:319
  449.7 59.2 %reduce-scatter.7.cloned.1.call-start = ((), (), s32[]{:S(2)}) async-start(), calls=%async_computation.5 | async-start | bytes 983040 | tf_op jit(solution)/shard_map/reduce_scatter | solution.py:204
  450.6 83.6 %reduce-scatter.11.cloned.1.call-start = ((), (), s32[]{:S(2)}) async-start(), calls=%async_computation.7 | async-start | bytes 491520 | tf_op jit(solution)/shard_map/reduce_scatter | solution.py:341
  489.0 3.1 collective-permute-start.3
  494.5 127.3 %all-reduce.32.cloned.1.call-start = ((), (), s32[]{:S(2)}) async-start(), calls=%async_computation.10 | async-start | bytes 8650752 | tf_op jit(solution)/shard_map/psum | solution.py:426
  497.9 36.3 %slice-start.1 = ((bf16[256,640]{1,0:T(8,128)(2,1)}), bf16[256,256]{1,0:T(8,128)(2,1)S(1)}, s32[]{:S(2)}) async-start(bf16[256,640]{1,0:T(8,128)(2,1)} %copy-done.38), calls=%async_computation.14 | async-start | bytes 262144 | tf_op jit(solution)/shard_map/slice | solution.py:337
  509.9 41.0 %copy-start.86 = (bf16[1,768,6]{1,2,0:T(8,128)(2,1)S(1)}, bf16[1,768,6]{1,2,0:T(8,128)(2,1)}, u32[]{:S(2)}) copy-start(bf16[1,768,6]{1,2,0:T(8,128)(2,1)} %fusion.81) | copy-start | bytes 27652
  509.9 41.0 %copy-start.139 = (bf16[1,768,6]{1,2,0:T(8,128)(2,1)S(1)}, bf16[1,768,6]{1,2,0:T(8,128)(2,1)}, u32[]{:S(2)}) copy-start(bf16[1,768,6]{1,2,0:T(8,128)(2,1)} %fusion.80) | copy-start | bytes 27652
  509.9 41.0 %slice-start.2 = ((bf16[1,640]{1,0:T(2,128)(2,1)}), bf16[1,384]{1,0:T(2,128)(2,1)S(1)}, s32[]{:S(2)}) async-start(bf16[1,640]{1,0:T(2,128)(2,1)} %copy-done.158), calls=%async_computation.15 | async-start | bytes 3072 | tf_op jit(solution)/shard_map/slice | solution.py:366
  509.9 41.0 %slice-start.3 = ((bf16[1,640]{1,0:T(2,128)(2,1)}), bf16[1,384]{1,0:T(2,128)(2,1)S(1)}, s32[]{:S(2)}) async-start(bf16[1,640]{1,0:T(2,128)(2,1)} %copy-done.159), calls=%async_computation.16 | async-start | bytes 3072 | tf_op jit(solution)/shard_map/slice | solution.py:366
  509.9 41.0 %copy-start.160 = (bf16[1,384]{1,0:T(2,128)(2,1)S(1)}, bf16[1,384]{1,0:T(2,128)(2,1)}, u32[]{:S(2)}) copy-start(bf16[1,384]{1,0:T(2,128)(2,1)} %stack.257) | copy-start | bytes 2308
  509.9 41.0 %copy-start.168 = (bf16[6]{0:T(256)(128)(2,1)S(1)}, bf16[6]{0:T(256)(128)(2,1)}, u32[]{:S(2)}) copy-start(bf16[6]{0:T(256)(128)(2,1)} %get-tuple-element.673) | copy-start | bytes 40
  509.9 41.0 %copy-start.169 = (bf16[6]{0:T(256)(128)(2,1)S(1)}, bf16[6]{0:T(256)(128)(2,1)}, u32[]{:S(2)}) copy-start(bf16[6]{0:T(256)(128)(2,1)} %get-tuple-element.671) | copy-start | bytes 40
  509.9 41.0 %copy-start.170 = (bf16[6]{0:T(256)(128)(2,1)S(1)}, bf16[6]{0:T(256)(128)(2,1)}, u32[]{:S(2)}) copy-start(bf16[6]{0:T(256)(128)(2,1)} %reduce_sum.470) | copy-start | bytes 40
  509.9 70.9 %copy-start.145 = (f32[256]{0:T(256)S(1)}, f32[256]{0:T(256)}, u32[]{:S(2)}) copy-start(f32[256]{0:T(256)} %copy-done.144) | copy-start | bytes 3076
  (172 other events, 1269.9 us)
Sparse Core Ops, SparseCore 0:
  28.5 28.1 all-gather.10
  79.1 28.0 reduce-scatter.4
  139.6 25.9 all-gather.12
  297.8 33.6 all-reduce.35
  341.3 21.0 reduce-scatter.8
  449.8 33.2 all-reduce.33
  486.0 22.8 reduce-scatter.6
  511.7 22.4 reduce-scatter.10
  539.3 82.4 all-reduce.31
where the time goes:
time: 644 us; the launch traced here: 637 us
  blocking collectives  208 us (32%)
  waiting for transfers between devices  134 us (21%)
  matrix products  97.5 us (15%)
  other arithmetic  95.7 us (15%)
  local copies, waits for them, and re-layouts  66.2 us (10%)
  between operations  17.2 us (3%)
  loops' own time  11.5 us (2%)
  starting transfers between devices  6.94 us (1%)
    all_gather x4, blocking collectives, carried_in(): lax.all_gather(part.astype(kind), axis)  53.4 us
    all_gather x2, blocking collectives, layer_forward(): lax.all_gather(resid_share + mixer_part, 'head', axis=0, tiled=True)  40.7 us
    psum x1, waiting for transfers between devices, per_device(): lax.psum(weight_grads[1].astype(jnp.bfloat16), 'seq').astype(jnp.float32)  39.8 us
    reduce_scatter x2, waiting for transfers between devices, layer_forward(): lax.psum_scatter(jnp.dot(outgoing, out_proj, preferred_element_type=jnp.f...  38.1 us
    psum x2, waiting for transfers between devices, layer_backward(): lax.psum(g_queries.astype(jnp.bfloat16), 'head').astype(jnp.float32)  32.6 us
    all_gather x2, blocking collectives, layer_backward(): lax.all_gather(normed_part.astype(jnp.bfloat16), 'head', axis=0, tiled=True)  30 us
    dynamic_slice x32, local copies, waits for them, and re-layouts, turn(): part[at].astype(own.dtype)  29.4 us
    another operation x19, other arithmetic  24.5 us
  transfers between devices with their start and end apart: 13, of which 10 were waited for; matrix products, arithmetic and copies ran while one was open for 14% of the time, Pallas kernels for 0%

commit v1 on v0

v1 whole, which is shorter than its diff:
```python
import functools

import jax
import jax.numpy as jnp
from jax import lax
from jax.experimental import pallas as pl
from jax.experimental.pallas import tpu as pltpu
from jax.sharding import PartitionSpec as P

P_SIZE = 64
N = 128
LAYERS = 2
EPS = 1e-05
LANES = 128
HALO = 8
TH = 16
F32 = jnp.float32
BF = jnp.bfloat16
HI = lax.Precision.HIGHEST


def dot(a, b, dims=((1,), (0,)), precision=None):
    return lax.dot_general(a, b, (dims, ((), ())), preferred_element_type=F32, precision=precision)


NT = ((1,), (1,))
TN = ((0,), (0,))


def iotas(rows, cols):
    return (
        lax.broadcasted_iota(jnp.int32, (rows, cols), 0),
        lax.broadcasted_iota(jnp.int32, (rows, cols), 1),
    )


def tri(rows, lower=True):
    r, c = iotas(rows, rows)
    return jnp.where(c <= r if lower else c >= r, 1.0, 0.0)


def flags8(flags_ref):
    return jnp.broadcast_to(flags_ref[...].astype(F32), (8, flags_ref.shape[1])).astype(BF)


def seg_col(flags_ref):
    t = flags_ref.shape[1]
    return dot(tri(t).astype(BF), flags8(flags_ref), NT)[:, 0:1]


def seg_row(flags_ref):
    t = flags_ref.shape[1]
    return dot(flags8(flags_ref), tri(t, False).astype(BF))[0:1, :]


def windows(flags_ref, taps):
    t = flags_ref.shape[1]
    r, c = iotas(t, t)
    fl = flags8(flags_ref)
    out = [None]
    for d in range(1, taps):
        band = jnp.where((c <= r) & (c > r - d), 1.0, 0.0).astype(BF)
        out.append(jnp.where(dot(band, fl, NT)[:, 0:1] == 0.0, 1.0, 0.0))
    return out


def spread(cols, heads):
    rows = cols.shape[0]
    return jnp.concatenate(
        [jnp.broadcast_to(cols[:, h : h + 1], (rows, P_SIZE)) for h in range(heads)], axis=1
    )


def head_sum(z):
    r, c = iotas(z.shape[1], LANES)
    lo = c * P_SIZE
    pick = jnp.where((r >= lo) & (r < lo + P_SIZE), 1.0, 0.0)
    return dot(z, pick, precision=HI)


def sigmoid(v):
    return 1.0 / (1.0 + jnp.exp(-v))


def softplus(v):
    return jnp.maximum(v, 0.0) + jnp.log(1.0 + jnp.exp(-jnp.abs(v)))


def two(col, width):
    rows = col.shape[0]
    _, c = iotas(rows, width)
    high = col.astype(BF).astype(F32)
    low = col - high
    return jnp.where(c == 0, high, jnp.where(c == 1, low, 0.0)).astype(BF)


def untwo(block):
    b = block.astype(F32)
    return b[:, 0:1] + b[:, 1:2]


def through_rows(row):
    r, _ = iotas(TH, row.shape[1])
    high = row.astype(BF).astype(F32)
    return jnp.where(r == 0, high, jnp.where(r == 1, row - high, 0.0)).astype(BF)


def closing_parts(cum, segc):
    t = cum.shape[0]
    last, seg_last = cum[t - 1 : t, :], segc[t - 1 : t, :]
    closing = jnp.exp(last - cum) * jnp.where(segc == seg_last, 1.0, 0.0)
    through = jnp.exp(last) * jnp.where(seg_last == 0.0, 1.0, 0.0)
    return closing, through


def norm_of(r, gain):
    inv = lax.rsqrt(jnp.mean(r * r, axis=1, keepdims=True) + EPS)
    return r * inv * gain


def at_rows(s_ref, k, rows):
    return pl.ds(pl.multiple_of(s_ref[k] * rows, rows), rows)


def k_project(layer, nh, refs):
    if layer == 0:
        stream, gain, wz, wx, wbc, wdt, gate, cin, dtr, normed = refs
        nm = norm_of(stream[...].astype(F32), gain[0:1, :]).astype(BF)
        normed[...] = nm
    else:
        s_ref, chunks, refs = refs[0], refs[1 : 1 + nh], refs[1 + nh :]
        wz, wx, wbc, wdt, gate, cin, dtr, normed, invc = refs
        rows, d = chunks[0].shape[0], normed.shape[1]
        for k in range(nh):
            normed[at_rows(s_ref, k, rows), :] = chunks[k][:, :d]
            both = jnp.broadcast_to(untwo(chunks[k][:, d:]), (rows, LANES))
            invc[at_rows(s_ref, k, rows), :] = both
        nm = normed[...]
    ch = wz.shape[1]
    gate[...] = dot(nm, wz[...])
    cin[:, :ch] = dot(nm, wx[...]).astype(BF)
    cin[:, ch:] = dot(nm, wbc[...]).astype(BF)
    dtr[...] = dot(nm, wdt[...])


def k_conv(layer, heads, raw_halo, refs):
    (halo, gain, cin, dtr, flags, wx, wbc, cx, cxb, cbc, cbcb, dtb, alog,
     act, ds, hc, step, cum, pay, ext) = refs
    t, cc = cin.shape
    ch = wx.shape[1]
    taps = cx.shape[1]
    hn = halo[...]
    if raw_halo:
        hn = norm_of(hn.astype(F32), gain[layer : layer + 1, :]).astype(BF)
    hx, hb = dot(hn, wx[...]).astype(BF), dot(hn, wbc[...]).astype(BF)
    hc[:, :ch] = hx
    hc[:, ch:] = hb
    ext[:HALO, :ch] = hx.astype(F32)
    ext[:HALO, ch:] = hb.astype(F32)
    ext[HALO:, :] = cin[...].astype(F32)
    valid = windows(flags, taps)
    for lo, hi, w, b in ((0, ch, cx, cxb), (ch, cc, cbc, cbcb)):
        v = b[layer : layer + 1, :] + w[layer, taps - 1 : taps, :] * ext[HALO:, lo:hi]
        for d in range(1, taps):
            tap = w[layer, taps - 1 - d : taps - d, :]
            v = v + tap * (ext[HALO - d : HALO - d + t, lo:hi] * valid[d])
        sig = sigmoid(v)
        act[:, lo:hi] = (v * sig).astype(BF)
        ds[:, lo:hi] = (sig * (1.0 + v * (1.0 - sig))).astype(BF)
    st = softplus(dtr[...] + dtb[layer : layer + 1, :])
    rate = -jnp.exp(alog[layer : layer + 1, :])
    cm = dot(tri(t), st * rate, precision=HI)
    step[...] = st
    cum[...] = cm
    closing, through = closing_parts(cm, seg_col(flags))
    x = act[:, :ch].astype(F32)
    xs = (x * spread(st * closing, heads)).astype(BF)
    pay[:N, :] = dot(act[:, ch : ch + N], xs, TN).astype(BF)
    pay[N:, :] = through_rows(spread(through, heads))


def k_combine(first, last, refs):
    flag, own, got = refs[0], refs[1], refs[2]
    refs = refs[3:]
    if not first:
        pre, q = refs[0], refs[1]
        refs = refs[2:]
    mine = flag[0] == 1
    s_own, s_got = own[:N, :].astype(F32), got[:N, :].astype(F32)
    t_own = own[N : N + 1, :].astype(F32) + own[N + 1 : N + 2, :].astype(F32)
    t_got = got[N : N + 1, :].astype(F32) + got[N + 1 : N + 2, :].astype(F32)
    if first:
        new_pre = jnp.where(mine, s_got, 0.0)
        new_q = jnp.where(mine, t_got, 1.0)
    else:
        qv = q[0:1, :]
        new_pre = pre[...] + jnp.where(mine, qv * s_got, 0.0)
        new_q = qv * jnp.where(mine, t_got, 1.0)
    refs[0][...] = new_pre.astype(refs[0].dtype)
    if not last:
        refs[1][...] = jnp.broadcast_to(new_q, (8, new_q.shape[1]))
        total = refs[2]
        total[:N, :] = (
            jnp.where(mine, s_own, s_got)
            + jnp.where(mine, t_own, t_got) * jnp.where(mine, s_got, s_own)
        ).astype(BF)
        total[N:, :] = through_rows(t_own * t_got)


def decay_of(cum_col, cum_row, allowed):
    return jnp.exp(jnp.where(allowed, cum_col - cum_row, -1e30))


def k_inside(heads, refs):
    act, step, cum, flags, yin = refs
    t = act.shape[0]
    ch = yin.shape[1]
    r, c = iotas(t, t)
    allowed = (c <= r) & (seg_col(flags) == seg_row(flags))
    scores = dot(act[:, ch + N :], act[:, ch : ch + N], NT)
    cm = cum[...]
    cmt = cm.T
    xs = (act[:, :ch].astype(F32) * spread(step[...], heads)).astype(BF)
    for h in range(heads):
        m = decay_of(cm[:, h : h + 1], cmt[h : h + 1, :], allowed) * scores
        cols = slice(h * P_SIZE, (h + 1) * P_SIZE)
        yin[:, cols] = dot(m.astype(BF), xs[:, cols])


def k_output(layer, heads, nh, refs):
    s_ref, pre, act, cum, flags, yin, gate, gain, skip, wo = refs[:10]
    refs = refs[10:]
    final = layer == LAYERS - 1
    if final:
        low = refs[0]
        refs = refs[1:]
    y0, refs = refs[0], refs[1:]
    chunks, refs = refs[:nh], refs[nh:]
    ch = yin.shape[1]
    d = wo.shape[1]
    opening = jnp.exp(cum[...]) * jnp.where(seg_col(flags) == 0.0, 1.0, 0.0)
    y = yin[...] + dot(act[:, ch + N :], pre[...]) * spread(opening, heads)
    y0[...] = y
    mixed = y + spread(skip[layer : layer + 1, :], heads) * act[:, :ch].astype(F32)
    gi = gate[...]
    gated = mixed * (gi * sigmoid(gi))
    sq = jnp.sum(gated * gated, axis=1, keepdims=True)
    scaled = gated * gain[layer : layer + 1, :]
    scratch = refs[-1]
    scratch[:, :d] = dot(scaled.astype(BF), wo[...]).astype(BF)
    scratch[:, d:] = two(sq, LANES)
    rows = chunks[0].shape[0]
    for k in range(nh):
        chunks[k][...] = scratch[at_rows(s_ref, k, rows), :]
    if final:
        gout, small = refs[0], refs[1]
        go = dot(low[...], wo[...], NT)
        gout[...] = go
        cross = jnp.sum(go * scaled, axis=1, keepdims=True)
        t = sq.shape[0]
        _, c = iotas(t, LANES)
        cols = jnp.where(c == 0, sq, jnp.where(c == 1, cross, 0.0))
        small[...] = cols.T[:8, :]


def k_stream(layer, nh, refs):
    s_ref, parts, refs = refs[0], refs[1 : 1 + nh], refs[1 + nh :]
    own, gain, width, r_out, tot_out, pay = refs[:3] + refs[3:]
    rows, wide = parts[0].shape
    d = wide - LANES
    total = parts[0][:, :d].astype(F32)
    sq = untwo(parts[0][:, d:])
    for p in parts[1:]:
        total = total + p[:, :d].astype(F32)
        sq = sq + untwo(p[:, d:])
    inv = lax.rsqrt(sq * width[0] + EPS)
    r = own[at_rows(s_ref, 0, rows), :].astype(F32) + total * inv
    r_out[...] = r
    tot_out[...] = total
    pay[:, :d] = norm_of(r, gain[layer + 1 : layer + 2, :]).astype(BF)
    pay[:, d:] = two(inv, LANES)


def k_stream_last(nh, refs):
    s_ref, parts, refs = refs[0], refs[1 : 1 + nh], refs[1 + nh :]
    own, width, r_out = refs
    rows, wide = parts[0].shape
    d = wide - LANES
    total = parts[0][:, :d].astype(F32)
    sq = untwo(parts[0][:, d:])
    for p in parts[1:]:
        total = total + p[:, :d].astype(F32)
        sq = sq + untwo(p[:, d:])
    r_out[...] = (own[...] + total * lax.rsqrt(sq * width[0] + EPS)).astype(BF)


def k_join(nh, refs):
    s_ref, parts, out = refs[0], refs[1 : 1 + nh], refs[1 + nh]
    rows = parts[0].shape[0]
    for k in range(nh):
        out[at_rows(s_ref, k, rows), :] = parts[k][...].astype(F32)


def k_gate_back(layer, heads, nh, refs):
    final = layer == LAYERS - 1
    if final:
        smalls, refs = refs[:nh], refs[nh:]
        gout, width, gain, y0, gate, act, cum, flags, skip = refs[:9]
        refs = refs[9:]
        acc = smalls[0][...]
        for s in smalls[1:]:
            acc = acc + s[...]
        t = acc.shape[1]
        cols = jnp.concatenate([acc, jnp.zeros((LANES - 8, t), F32)], axis=0).T
        inv = lax.rsqrt(cols[:, 0:1] * width[0] + EPS)
        cross = cols[:, 1:2]
        go = gout[...]
        pay, gm, lowgate, og, small = refs
    else:
        s_ref, chunks, refs = refs[0], refs[1 : 1 + nh], refs[1 + nh :]
        wo, invc, width, gain, y0, gate, act, cum, flags, skip = refs[:10]
        pay, gm, lowgate, og, small, low, crs = refs[10:]
        rows, d = chunks[0].shape[0], wo.shape[1]
        for k in range(nh):
            low[at_rows(s_ref, k, rows), :] = chunks[k][:, :d]
            both = jnp.broadcast_to(untwo(chunks[k][:, d:]), (rows, LANES))
            crs[at_rows(s_ref, k, rows), :] = both
        cross = crs[:, 0:1]
        inv = invc[:, 0:1]
        go = dot(low[...], wo[...], NT)
    ch = y0.shape[1]
    gn = gain[layer : layer + 1, :]
    x = act[:, :ch].astype(F32)
    mixed = y0[...] + spread(skip[layer : layer + 1, :], heads) * x
    gi = gate[...]
    sig = sigmoid(gi)
    silu = gi * sig
    gated = mixed * silu
    ginv = gated * inv
    og[...] = (ginv * gn).astype(BF)
    g_gated = inv * (gn * go) - ginv * (inv * inv * cross * width[0])
    g_mixed = g_gated * silu
    lowgate[...] = (g_gated * mixed * (sig * (1.0 + gi * (1.0 - sig)))).astype(BF)
    gm[...] = g_mixed.astype(BF)
    segc = seg_col(flags)
    cm = cum[...]
    opening = jnp.exp(cm) * jnp.where(segc == 0.0, 1.0, 0.0)
    _, through = closing_parts(cm, segc)
    grad = dot(act[:, ch + N :], (g_mixed * spread(opening, heads)).astype(BF), TN)
    pay[:N, :] = grad.astype(BF)
    pay[N:, :] = through_rows(spread(through, heads))
    r, _ = iotas(8, ch)
    row0 = jnp.sum(go * ginv, axis=0, keepdims=True)
    row1 = jnp.sum(g_mixed * x, axis=0, keepdims=True)
    small[...] = jnp.where(r == 0, row0, jnp.where(r == 1, row1, 0.0))


def k_inside_back(heads, refs):
    (act, step, cum, flags, gm, pre, low, og, normed, lowgate,
     dxs, dbc, wout, wz) = refs
    t, ch = gm.shape
    r, c = iotas(t, t)
    segc = seg_col(flags)
    allowed = (c <= r) & (segc == seg_row(flags))
    keys, queries = act[:, ch : ch + N], act[:, ch + N :]
    scores = dot(queries, keys, NT)
    cm = cum[...]
    cmt = cm.T
    xs = (act[:, :ch].astype(F32) * spread(step[...], heads)).astype(BF)
    dy = gm[...]
    acc = jnp.zeros((t, t), F32)
    for h in range(heads):
        cols = slice(h * P_SIZE, (h + 1) * P_SIZE)
        decay = decay_of(cm[:, h : h + 1], cmt[h : h + 1, :], allowed)
        m = (decay * scores).astype(BF)
        dxs[:, cols] = dot(m, dy[:, cols], TN)
        acc = acc + dot(dy[:, cols], xs[:, cols], NT) * decay
    low_s = acc.astype(BF)
    dbc[:, :N] = dot(low_s, queries, TN)
    opening = jnp.exp(cm) * jnp.where(segc == 0.0, 1.0, 0.0)
    carried = (dy.astype(F32) * spread(opening, heads)).astype(BF)
    dbc[:, N:] = dot(low_s, keys) + dot(carried, pre[...], NT)
    wout[...] = dot(og[...], low[...], TN).astype(BF)
    wz[...] = dot(normed[...], lowgate[...], TN).astype(BF)


def k_state_back(layer, heads, refs):
    (g, pre, act, step, cum, dtr, flags, gm, y0, dxs, dbc, ds, cin, hc, cx, cbc, skip, dtb, alog,
     gb, gh, lowraw, small, ext, u_ref) = refs
    t, ch = gm.shape
    cc = cin.shape[1]
    taps = cx.shape[1]
    segc = seg_col(flags)
    cm = cum[...]
    st = step[...]
    closing, through = closing_parts(cm, segc)
    x = act[:, :ch].astype(F32)
    st_ch = spread(st, heads)
    clo_ch = spread(closing, heads)
    xs = (x * st_ch).astype(BF)
    xsf = xs.astype(F32)
    gst = g[...]
    gb16 = gst.astype(BF)
    keys = act[:, ch : ch + N]
    dwc = dot(keys, gb16) * clo_ch
    dkeys = dbc[:, :N] + dot((xsf * clo_ch).astype(BF), gb16, NT)
    dx_all = dxs[...] + dwc
    gmf = gm[...].astype(F32)
    z = head_sum(x * dx_all)
    dcum = head_sum(gmf * y0[...] - xsf * dx_all)
    at_last = jnp.sum(head_sum(xsf * dwc), axis=0, keepdims=True)
    keep = jnp.sum(gst * pre[...].astype(F32), axis=0, keepdims=True)
    at_last = at_last + through * head_sum(jnp.broadcast_to(keep, (8, ch)))[0:1, :]
    ddecay = dot(tri(t, False), dcum, precision=HI) + at_last
    rate = -jnp.exp(alog[layer : layer + 1, :])
    graw = (z + ddecay * rate) * sigmoid(dtr[...] + dtb[layer : layer + 1, :])
    lowraw[...] = graw.astype(BF)
    g_alog = jnp.sum(ddecay * st, axis=0, keepdims=True) * rate
    g_dtb = jnp.sum(graw, axis=0, keepdims=True)
    ext[:HALO, :] = hc[...].astype(F32)
    ext[HALO:, :] = cin[...].astype(F32)
    gv_x = (dx_all * st_ch + spread(skip[layer : layer + 1, :], heads) * gmf)
    valid = windows(flags, taps)
    for lo, hi, w, val in (
        (0, ch, cx, gv_x),
        (ch, ch + N, cbc, dkeys),
        (ch + N, cc, cbc, dbc[:, N:]),
    ):
        wl = lo if lo < ch else lo - ch
        gv = val * ds[:, lo:hi].astype(F32)
        small[4:5, lo:hi] = jnp.sum(gv, axis=0, keepdims=True)
        total = None
        for d in range(taps):
            u = gv if d == 0 else gv * valid[d]
            k = taps - 1 - d
            small[k : k + 1, lo:hi] = jnp.sum(
                u * ext[HALO - d : HALO - d + t, lo:hi], axis=0, keepdims=True
            )
            u_ref[0:HALO, lo:hi] = jnp.zeros((HALO, hi - lo), F32)
            u_ref[HALO : HALO + t, lo:hi] = u
            u_ref[HALO + t :, lo:hi] = jnp.zeros((HALO, hi - lo), F32)
            term = w[layer, k : k + 1, wl : wl + hi - lo] * u_ref[d : d + t + HALO, lo:hi]
            total = term if total is None else total + term
        gh[:, lo:hi] = total[:HALO, :]
        gb[:, lo:hi] = total[HALO:, :]
    small[5:8, :] = jnp.zeros((3, cc), F32)
    small[5:6, :LANES] = g_dtb
    small[6:7, :LANES] = g_alog


def k_back_project(refs):
    lowgate, gb, lowraw, wz, wx, wbc, wdt, part = refs
    ch = wz.shape[1]
    part[...] = (
        dot(lowgate[...], wz[...], NT)
        + dot(gb[:, :ch].astype(BF), wx[...], NT)
        + dot(gb[:, ch:].astype(BF), wbc[...], NT)
        + dot(lowraw[...], wdt[...], NT)
    )


def k_back_fix(nh, refs):
    s_ref, part, ret, wx, wbc = refs[:5]
    chunks, scratch = refs[5 : 5 + nh], refs[5 + nh]
    t = part.shape[0]
    ch = wx.shape[1]
    scratch[...] = part[...].astype(BF)
    low = ret[...].astype(BF)
    fix = dot(low[:, :ch], wx[...], NT) + dot(low[:, ch:], wbc[...], NT)
    fix = jnp.concatenate([jnp.zeros_like(fix), fix], axis=0)
    scratch[t - 2 * HALO :, :] = (part[t - 2 * HALO :, :] + fix).astype(BF)
    rows = chunks[0].shape[0]
    for k in range(nh):
        chunks[k][...] = scratch[at_rows(s_ref, k, rows), :]


def k_weights(refs):
    normed, gb, ret, lowraw, wx, wbc, wdt, scratch = refs
    t = gb.shape[0]
    ch = wx.shape[1]
    scratch[...] = gb[...].astype(BF)
    tail = gb[t - 2 * HALO :, :]
    fix = jnp.concatenate([jnp.zeros_like(ret[...]), ret[...]], axis=0)
    scratch[t - 2 * HALO :, :] = (tail + fix).astype(BF)
    nm = normed[...]
    wx[...] = dot(nm, scratch[:, :ch], TN).astype(BF)
    wbc[...] = dot(nm, scratch[:, ch:], TN).astype(BF)
    wdt[...] = dot(nm, lowraw[...], TN).astype(BF)


def k_norm_back(layer, nh, refs):
    s_ref, parts, refs = refs[0], refs[1 : 1 + nh], refs[1 + nh :]
    final = layer == LAYERS - 1
    if layer > 0:
        r_own, g_in, gain, total, g_out, gng, pay = refs
    else:
        r_own, g_in, gain, gng, pay = refs
    rows, d = parts[0].shape
    gn = parts[0][...].astype(F32)
    for p in parts[1:]:
        gn = gn + p[...].astype(F32)
    r = r_own[...] if layer > 0 else r_own[at_rows(s_ref, 0, rows), :].astype(F32)
    old = g_in[at_rows(s_ref, 0, rows), :].astype(F32) if final else g_in[...]
    inv = lax.rsqrt(jnp.mean(r * r, axis=1, keepdims=True) + EPS)
    ri = r * inv
    gg = gn * gain[layer : layer + 1, :]
    new = old + inv * (gg - ri * jnp.mean(gg * ri, axis=1, keepdims=True))
    gng[...] = jnp.broadcast_to(jnp.sum(gn * ri, axis=0, keepdims=True), (8, d))
    if layer > 0:
        g_out[...] = new
        low = new.astype(BF)
        pay[:, :d] = low
        cross = jnp.sum(low.astype(F32) * total[...], axis=1, keepdims=True)
        pay[:, d:] = two(cross, LANES)
    else:
        pay[...] = new.astype(BF)


SMEM = pl.BlockSpec(memory_space=pltpu.SMEM)


class Layered:
    def __init__(self, array, *lead):
        self.array, self.lead = array, lead


def call(body, name, args, outs, scratch=(), flops=0):
    specs, arrays = [], []
    size = 0
    for a in args:
        if isinstance(a, Layered):
            rest = a.array.shape[len(a.lead) :]
            lead = a.lead
            specs.append(
                pl.BlockSpec(
                    (None,) * len(lead) + rest,
                    functools.partial(lambda lead, n, i: lead + (0,) * n, lead, len(rest)),
                )
            )
            arrays.append(a.array)
            count = 1
            for s in rest:
                count *= s
            size += count * a.array.dtype.itemsize
        elif a.dtype == jnp.int32 and a.ndim == 1 or a.ndim == 1:
            specs.append(SMEM)
            arrays.append(a)
        else:
            specs.append(pl.BlockSpec(a.shape, functools.partial(lambda n, i: (0,) * n, a.ndim)))
            arrays.append(a)
            size += a.size * a.dtype.itemsize
    for s, t in outs:
        count = 1
        for k in s:
            count *= k
        size += count * jnp.dtype(t).itemsize

    def kernel(*refs):
        body(refs)

    return pl.pallas_call(
        kernel,
        out_shape=[jax.ShapeDtypeStruct(s, t) for s, t in outs],
        grid=(1,),
        in_specs=specs,
        out_specs=[
            pl.BlockSpec(s, functools.partial(lambda n, i: (0,) * n, len(s))) for s, _ in outs
        ],
        scratch_shapes=[pltpu.VMEM(s, t) for s, t in scratch],
        compiler_params=pltpu.CompilerParams(vmem_limit_bytes=48 << 20),
        cost_estimate=pl.CostEstimate(flops=flops, bytes_accessed=size, transcendentals=0),
        name=name,
    )(*arrays)


def swap(array, axis, by):
    count = lax.axis_size(axis)
    return lax.ppermute(array, axis, [(i, i ^ by) for i in range(count)])


def passed(array, axis, by):
    count = lax.axis_size(axis)
    return lax.ppermute(array, axis, [(i, i + by) for i in range(count) if 0 <= i + by < count])


def scan_blocks(pay, forward, out_type):
    count = lax.axis_size("seq")
    place = lax.axis_index("seq")
    ch = pay.shape[1]
    pre = q = None
    by = 1
    while by < count:
        got = swap(pay, "seq", by)
        upper = (place // by) % 2
        flag = jnp.reshape(upper if forward else 1 - upper, (1,)).astype(jnp.int32)
        first, last = by == 1, by * 2 >= count
        outs = [((N, ch), out_type if last else F32)]
        if not last:
            outs += [((8, ch), F32), ((N + TH, ch), BF)]
        args = [flag, pay, got] + ([] if first else [pre, q])
        res = call(
            functools.partial(k_combine, first, last), "combine", args, outs
        )
        pre = res[0]
        if not last:
            q, pay = res[1], res[2]
        by *= 2
    return pre


def to_shares(chunks):
    nh = lax.axis_size("head")
    return [chunks[0]] + [swap(chunks[k], "head", k) for k in range(1, nh)]


def from_shares(share):
    nh = lax.axis_size("head")
    return [share] + [swap(share, "head", k) for k in range(1, nh)]


def layer_forward(layer, src, halo_raw, prm, flags, order, width, cot):
    nh = lax.axis_size("head")
    norm_gain, in_zx, in_bc, in_dt, dtb, alog, skip, cx, cxb, cbc, cbcb, gate_gain, out_proj = prm
    d, ch = in_zx.shape[2], in_zx.shape[3]
    heads = ch // P_SIZE
    t = flags.shape[1]
    cc = ch + 2 * N
    wz, wx = Layered(in_zx, layer, 0), Layered(in_zx, layer, 1)
    wbc, wdt, wo = Layered(in_bc, layer), Layered(in_dt, layer), Layered(out_proj, layer)
    outs = [((t, ch), F32), ((t, cc), BF), ((t, LANES), F32), ((t, d), BF)]
    work = 2 * t * d * (2 * ch + 2 * N + LANES)
    if layer == 0:
        halo = passed(halo_raw, "seq", 1)
        gate, cin, dtr, normed = call(
            functools.partial(k_project, 0, nh), "project0",
            [src, norm_gain, wz, wx, wbc, wdt], outs, flops=work,
        )
        invc = None
    else:
        rows = src[0].shape[0]
        tail = jnp.zeros((HALO, d), BF)
        for k in range(nh):
            tail = jnp.where(order[k] == nh - 1, src[k][rows - HALO :, :d], tail)
        halo = passed(tail, "seq", 1)
        gate, cin, dtr, normed, invc = call(
            functools.partial(k_project, layer, nh), "project1",
            [order, *src, wz, wx, wbc, wdt], outs + [((t, LANES), F32)], flops=work,
        )
    act, ds, hc, step, cum, pay = call(
        functools.partial(k_conv, layer, heads, layer == 0), "conv",
        [halo, norm_gain, cin, dtr, flags, wx, wbc, cx, cxb, cbc, cbcb, dtb, alog],
        [((t, cc), BF), ((t, cc), BF), ((HALO, cc), BF), ((t, LANES), F32), ((t, LANES), F32),
         ((N + TH, ch), BF)],
        [((t + HALO, cc), F32)],
        flops=2 * t * N * ch,
    )
    pre = scan_blocks(pay, True, BF)
    (yin,) = call(
        functools.partial(k_inside, heads), "inside", [act, step, cum, flags], [((t, ch), F32)],
        flops=2 * t * t * ch * 2,
    )
    final = layer == LAYERS - 1
    rows = t // nh
    outs = [((t, ch), F32)] + [((rows, d + LANES), BF)] * nh
    args = [order, pre, act, cum, flags, yin, gate, gate_gain, skip, wo]
    if final:
        args.append(cot)
        outs += [((t, ch), F32), ((8, t), F32)]
    res = call(
        functools.partial(k_output, layer, heads, nh), "output", args, outs,
        [((t, d + LANES), BF)], flops=2 * t * ch * d,
    )
    stored = dict(
        gate=gate, cin=cin, dtr=dtr, normed=normed, act=act, ds=ds, hc=hc, step=step, cum=cum,
        pre=pre, y0=res[0],
    )
    if final:
        stored["gout"], stored["small"] = res[1 + nh], res[2 + nh]
    return res[1 : 1 + nh], invc, stored


def layer_backward(layer, sv, low_src, invc, prm, flags, order, width, own):
    nh = lax.axis_size("head")
    norm_gain, in_zx, in_bc, in_dt, dtb, alog, skip, cx, cxb, cbc, cbcb, gate_gain, out_proj = prm
    d, ch = in_zx.shape[2], in_zx.shape[3]
    heads = ch // P_SIZE
    t = flags.shape[1]
    cc = ch + 2 * N
    rows = t // nh
    wz, wx = Layered(in_zx, layer, 0), Layered(in_zx, layer, 1)
    wbc, wdt, wo = Layered(in_bc, layer), Layered(in_dt, layer), Layered(out_proj, layer)
    outs = [((N + TH, ch), BF), ((t, ch), BF), ((t, ch), BF), ((t, ch), BF), ((8, ch), F32)]
    common = [gate_gain, sv["y0"], sv["gate"], sv["act"], sv["cum"], flags, skip]
    body = functools.partial(k_gate_back, layer, heads, nh)
    if layer == LAYERS - 1:
        pay, gm, lowgate, og, small_g = call(
            body, "gateback1",
            [*from_shares(sv["small"]), sv["gout"], width, *common], outs, flops=2 * t * N * ch,
        )
        low = low_src
    else:
        pay, gm, lowgate, og, small_g, low = call(
            body, "gateback0",
            [order, *low_src, wo, invc, width, *common], outs + [((t, d), BF)],
            [((t, LANES), F32)], flops=2 * t * ch * d,
        )
    state_grad = scan_blocks(pay, False, F32)
    dxs, dbc, w_out, w_z = call(
        functools.partial(k_inside_back, heads), "insideback",
        [sv["act"], sv["step"], sv["cum"], flags, gm, sv["pre"], low, og, sv["normed"], lowgate],
        [((t, ch), F32), ((t, 2 * N), F32), ((ch, d), BF), ((d, ch), BF)],
        flops=2 * t * t * ch * 4 + 4 * t * d * ch,
    )
    gb, gh, lowraw, small = call(
        functools.partial(k_state_back, layer, heads), "stateback",
        [state_grad, sv["pre"], sv["act"], sv["step"], sv["cum"], sv["dtr"], flags, gm, sv["y0"],
         dxs, dbc, sv["ds"], sv["cin"], sv["hc"], cx, cbc, skip, dtb, alog],
        [((t, cc), F32), ((HALO, cc), F32), ((t, LANES), BF), ((8, cc), F32)],
        [((t + HALO, cc), F32), ((t + 2 * HALO, cc), F32)],
        flops=4 * t * N * ch,
    )
    ret = passed(gh, "seq", -1)
    (part,) = call(
        k_back_project, "backproject", [lowgate, gb, lowraw, wz, wx, wbc, wdt], [((t, d), F32)],
        flops=2 * t * d * (2 * ch + 3 * N),
    )
    chunks = call(
        functools.partial(k_back_fix, nh), "backfix", [order, part, ret, wx, wbc],
        [((rows, d), BF)] * nh, [((t, d), BF)], flops=2 * 2 * HALO * d * cc,
    )
    parts = to_shares(chunks)
    w_x, w_bc, w_dt = call(
        k_weights, "weights", [sv["normed"], gb, ret, lowraw],
        [((d, ch), BF), ((d, 2 * N), BF), ((d, LANES), BF)], [((t, cc), BF)],
        flops=2 * t * d * (ch + 3 * N),
    )
    body = functools.partial(k_norm_back, layer, nh)
    if layer > 0:
        r_own, g_in, total = own
        g_own, gng, share = call(
            body, "normback1", [order, *parts, r_own, g_in, norm_gain, total],
            [((rows, d), F32), ((8, d), F32), ((rows, d + LANES), BF)],
        )
    else:
        r_own, g_in = own
        gng, share = call(
            body, "normback0", [order, *parts, r_own, g_in, norm_gain],
            [((8, d), F32), ((rows, d), BF)],
        )
        g_own = None
    grads = dict(
        w_out=w_out, w_z=w_z, w_x=w_x, w_bc=w_bc, w_dt=w_dt, small=small, small_g=small_g,
        gng=gng[0],
    )
    return from_shares(share), g_own, grads


def summed(grads, heads):
    small, small_g = grads["small"], grads["small_g"]
    ch = small_g.shape[1]
    g_skip = jnp.sum(small_g[1].reshape(heads, P_SIZE), axis=1)
    over_seq = [grads["w_z"], grads["w_x"], grads["w_dt"][:, :heads], grads["w_out"]]
    over_seq = [lax.psum(a, "seq").astype(F32) for a in over_seq]
    w_bc = lax.psum(grads["w_bc"], ("seq", "head")).astype(F32)
    flat = lax.psum(
        jnp.concatenate(
            [small[:5, :ch].reshape(-1), small_g[0], g_skip, small[5, :heads], small[6, :heads]]
        ),
        "seq",
    )
    both = lax.psum(
        jnp.concatenate([small[:5, ch:].reshape(-1), grads["gng"]]), ("seq", "head")
    )
    w_z, w_x, w_dt, w_out = over_seq
    x_rows = flat[: 5 * ch].reshape(5, ch)
    rest = flat[5 * ch :]
    bc = both[: 5 * 2 * N].reshape(5, 2 * N)
    return (
        both[5 * 2 * N :],
        jnp.stack([w_z, w_x]),
        w_bc,
        w_dt,
        rest[ch + heads : ch + 2 * heads],
        rest[ch + 2 * heads : ch + 3 * heads],
        rest[ch : ch + heads],
        x_rows[:4],
        x_rows[4],
        bc[:4],
        bc[4],
        rest[:ch],
        w_out,
    )


def per_device(
    stream, seq_flags, norm_gain, in_zx, in_bc, in_dt, dt_bias, a_log, skip_d, conv_x,
    conv_x_bias, conv_bc, conv_bc_bias, gate_gain, out_proj, cotangent,
):
    nh = lax.axis_size("head")
    t, d = stream.shape
    ch = in_zx.shape[3]
    heads = ch // P_SIZE
    rows = t // nh
    pad = LANES - heads
    flags = seq_flags.reshape(1, t)
    dt_pad = jnp.pad(in_dt, ((0, 0), (0, 0), (0, pad)))
    dtb, alog, skip = (jnp.pad(a, ((0, 0), (0, pad))) for a in (dt_bias, a_log, skip_d))
    prm = (
        norm_gain, in_zx, in_bc, dt_pad, dtb, alog, skip, conv_x, conv_x_bias, conv_bc,
        conv_bc_bias, gate_gain, out_proj,
    )
    order = lax.axis_index("head") ^ jnp.arange(nh, dtype=jnp.int32)
    width = jnp.full((1,), 1.0 / (ch * nh), F32)

    chunks, _, sv0 = layer_forward(
        0, stream, stream[t - HALO :], prm, flags, order, width, cotangent
    )
    r1, total0, share = call(
        functools.partial(k_stream, 0, nh), "stream0",
        [order, *to_shares(chunks), stream, norm_gain, width],
        [((rows, d), F32), ((rows, d), F32), ((rows, d + LANES), BF)],
    )
    chunks, invc0, sv1 = layer_forward(
        1, from_shares(share), None, prm, flags, order, width, cotangent
    )
    low, g1, grads1 = layer_backward(
        1, sv1, cotangent, None, prm, flags, order, width, (r1, cotangent, total0)
    )
    (out_share,) = call(
        functools.partial(k_stream_last, nh), "stream1",
        [order, *to_shares(chunks), r1, width], [((rows, d), BF)],
    )
    (output,) = call(
        functools.partial(k_join, nh), "join", [order, *from_shares(out_share)], [((t, d), F32)]
    )
    last, _, grads0 = layer_backward(
        0, sv0, low, invc0, prm, flags, order, width, (stream, g1)
    )
    (grad_stream,) = call(
        functools.partial(k_join, nh), "join", [order, *last], [((t, d), F32)]
    )
    per_layer = [summed(grads0, heads), summed(grads1, heads)]
    stacked = [jnp.stack(pair) for pair in zip(*per_layer)]
    return (output, grad_stream, *stacked)


def solution(mesh):
    placed = (
        P("seq", None),
        P("seq"),
        P(),
        P(None, None, None, "head"),
        P(),
        P(None, None, "head"),
        P(None, "head"),
        P(None, "head"),
        P(None, "head"),
        P(None, None, "head"),
        P(None, "head"),
        P(),
        P(),
        P(None, "head"),
        P(None, "head", None),
        P("seq", None),
    )
    return jax.shard_map(
        per_device,
        mesh=mesh,
        in_specs=placed,
        out_specs=(
            P("seq", None),
            P("seq", None),
            P(),
            P(None, None, None, "head"),
            P(),
            P(None, None, "head"),
            P(None, "head"),
            P(None, "head"),
            P(None, "head"),
            P(None, None, "head"),
            P(None, "head"),
            P(),
            P(),
            P(None, "head"),
            P(None, "head", None),
        ),
        check_vma=False,
    )
```

time: 644 us -> 513 us (0.80)
  blocking collectives: 208 us -> 91.2 us
  matrix products: 97.5 us -> 0 us
  other arithmetic: 95.7 us -> 18.9 us
  Pallas kernels: 0 us -> 54.3 us
  starting transfers between devices: 6.94 us -> 61 us
  local copies, waits for them, and re-layouts: 66.2 us -> 109 us
  waiting for transfers between devices: 134 us -> 157 us
  loops' own time: 11.5 us -> 0 us
    all_gather x10 -> x0, blocking collectives: 143 us -> none  [the longest x4 53.4 us: carried_in(): lax.all_gather(part.astype(kind), axis)]
    dot_general x52 -> x0, matrix products: 94.6 us -> none  [the longest x10 19.9 us: outer_t(): lax.dot_general(left, right, (((1,), (1,)), ((), ())), preferred_element_...]
    unnamed x380 -> x381, local copies, waits for them, and re-layouts: 8.37 us -> 83.4 us
    ppermute x4 -> x43, starting transfers between devices: 6.39 us -> 60.9 us  [the longest x39 53.8 us: swap(): return lax.ppermute(array, axis, [(i, i ^ by) for i in range(count)])]
    pallas_call x0 -> x38, Pallas kernels: none -> 54.3 us  [call(): pl.pallas_call(kernel, out_shape=[jax.ShapeDtypeStruct(s, t) for s, t in...]
    ppermute x4 -> x43, waiting for transfers between devices: 2.83 us -> 53.2 us  [the longest x39 52.2 us: swap(): return lax.ppermute(array, axis, [(i, i ^ by) for i in range(count)])]
    reduce_scatter x4 -> x0, waiting for transfers between devices: 41.8 us -> none  [the longest x2 38.1 us: layer_forward(): lax.psum_scatter(jnp.dot(outgoing, out_proj, preferred_element_type=jnp.f...]
    psum x3 -> x2, waiting for transfers between devices: 72.4 us -> 104 us  [the longest x1 75.8 us: summed(): over_seq = [lax.psum(a, 'seq').astype(F32) for a in over_seq]]
  transfers between devices with their start and end apart: 13 -> 45, of which waited for: 10 -> 21; matrix products, arithmetic and copies ran while one was open for 14% -> 7% of each run, Pallas kernels for 0% -> 5%
where the time goes in v1:
time: 513 us; the launch traced here: 510 us
  waiting for transfers between devices  157 us (31%)
  local copies, waits for them, and re-layouts  109 us (21%)
  blocking collectives  91.2 us (18%)
  starting transfers between devices  61 us (12%)
  Pallas kernels  54.3 us (11%)
  other arithmetic  18.9 us (4%)
  between operations  18.2 us (4%)
    unnamed x381, local copies, waits for them, and re-layouts  83.4 us
    psum x1, waiting for transfers between devices, summed(): over_seq = [lax.psum(a, 'seq').astype(F32) for a in over_seq]  75.8 us
    pallas_call x38, Pallas kernels, call(): pl.pallas_call(kernel, out_shape=[jax.ShapeDtypeStruct(s, t) for s, t in...  54.3 us
    ppermute x39, starting transfers between devices, swap(): return lax.ppermute(array, axis, [(i, i ^ by) for i in range(count)])  53.8 us
    ppermute x39, waiting for transfers between devices, swap(): return lax.ppermute(array, axis, [(i, i ^ by) for i in range(count)])  52.2 us
    psum x1, blocking collectives, summed(): lax.psum(jnp.concatenate([small[:5, ch:].reshape(-1), grads['gng']]), ('s...  38 us
    psum x1, waiting for transfers between devices, summed(): w_bc = lax.psum(grads['w_bc'], ('seq', 'head')).astype(F32)  28.2 us
    psum x1, blocking collectives, summed(): over_seq = [lax.psum(a, 'seq').astype(F32) for a in over_seq]  26.7 us
  transfers between devices with their start and end apart: 45, of which 21 were waited for; matrix products, arithmetic and copies ran while one was open for 7% of the time, Pallas kernels for 5%

profile of v1, /device:TPU:0, one launch (start us, length us, event | category | flops | bytes accessed | tf_op | source)
XLA Modules:
  0.0 509.8 jit_solution(1183959258393447441)
XLA Ops:
  8.6 3.0 collective-permute-start
  17.2 3.2 conv.2
  23.8 2.0 collective-permute-start.1
  32.1 3.6 collective-permute-done.2.refs_2_
  49.5 2.6 collective-permute-start.5
  54.0 6.6 %collective-permute-done.5.refs_3_ = bf16[64,896]{1,0:T(8,128)(2,1)S(1)} collective-permute-done((bf16[64,896]{1,0:T(8,128)(2,1)S(1)}, bf16[64,896]{1,0:T(8,128)(2,1)S(1)}, u32[]{:S(2)}, u32[]{:S(2)}) %collective-permute-start.5) | collective-permute-done | bytes 114720 | tf_op jit(solution)/shard_map/ppermute | solution.py:578
  70.4 4.5 collective-permute-done.8.refs_3_
  86.2 3.6 collective-permute-done.12.refs_2_
  96.5 2.3 collective-permute-start.22
  114.4 3.7 collective-permute-done.24.refs_2_
  137.3 3.0 insideback.2
  144.5 3.4 stateback.2
  152.2 2.7 collective-permute-start.28
  158.4 2.2 collective-permute-start.19
  160.6 4.5 collective-permute-done.28.refs_3_
  167.9 2.2 collective-permute-start.32
  172.3 2.5 collective-permute-start.18
  179.8 5.5 %collective-permute-done.18.refs_3_ = bf16[64,768]{1,0:T(8,128)(2,1)} collective-permute-done((bf16[64,768]{1,0:T(8,128)(2,1)}, bf16[64,768]{1,0:T(8,128)(2,1)}, u32[]{:S(2)}, u32[]{:S(2)}) %collective-permute-start.18) | collective-permute-done | bytes 98336 | tf_op jit(solution)/shard_map/ppermute | solution.py:578
  194.3 2.8 gateback0.1
  215.2 4.0 collective-permute-done.34.refs_2_
  233.8 3.0 insideback.3
  243.3 3.8 stateback.3
  253.7 26.5 %all-reduce.5 = (f32[2322]{0:T(1024)}, f32[2322]{0:T(1024)}) all-reduce(f32[2322]{0:T(1024)} %concatenate.15, f32[2322]{0:T(1024)} %concatenate.14), channel_id=1, replica_groups=mesh['seq'=8,'head'=4] {'seq'}, use_global_device_ids=true, to_apply=%region_13.14 | all-reduce | flops 4644 | bytes 37152 | tf_op jit(solution)/shard_map/psum | solution.py:765
  305.6 2.8 collective-permute-start.38
  310.1 26.7 %all-reduce.7 = (bf16[1,768,6]{2,1,0:T(8,128)(2,1)S(1)}, bf16[1,768,6]{2,1,0:T(8,128)(2,1)S(1)}) all-reduce(bf16[1,768,6]{2,1,0:T(8,128)(2,1)S(1)} %get-tuple-element.282, bf16[1,768,6]{2,1,0:T(8,128)(2,1)S(1)} %get-tuple-element.283), channel_id=1, replica_groups=mesh['seq'=8,'head'=4] {'seq'}, use_global_device_ids=true, to_apply=%region_9.10 | all-reduce | flops 9216 | bytes 36864 | tf_op jit(solution)/shard_map/psum | solution.py:763
  338.7 38.0 %all-reduce.4 = (f32[2048]{0:T(1024)S(1)}, f32[2048]{0:T(1024)S(1)}) all-reduce(f32[2048]{0:T(1024)S(1)} %get-tuple-element.279, f32[2048]{0:T(1024)S(1)} %get-tuple-element.278), channel_id=1, replica_groups=mesh['seq'=8,'head'=4] {'seq','head'}, use_global_device_ids=true, to_apply=%region_1.2 | all-reduce | flops 4096 | bytes 32768 | tf_op jit(solution)/shard_map/psum | solution.py:771
  378.4 2.0 collective-permute-start.41
  384.4 4.8 collective-permute-done.41.refs_3_
  390.7 28.2 %all-reduce.12.cloned.1.call-done = (bf16[1,768,256]{2,1,0:T(8,128)(2,1)}, bf16[1,768,256]{2,1,0:T(8,128)(2,1)}) async-done(((bf16[1,768,256]{2,1,0:T(8,128)(2,1)}, bf16[1,768,256]{2,1,0:T(8,128)(2,1)}), (bf16[1,768,256]{2,1,0:T(8,128)(2,1)}, bf16[1,768,256]{2,1,0:T(8,128)(2,1)})) %all-reduce.12.cloned.1.call-update) | async-done | bytes 786448 | tf_op jit(solution)/shard_map/psum | solution.py:764
  418.8 2.4 maximum_convert_fusion.2
  421.2 75.8 %all-reduce.14.cloned.1.call-done = (bf16[1,768,384]{2,1,0:T(8,128)(2,1)}, bf16[1,768,384]{2,1,0:T(8,128)(2,1)}, bf16[1,768,384]{2,1,0:T(8,128)(2,1)}, bf16[1,76...) async-done(((bf16[1,768,384]{2,1,0:T(8,128)(2,1)}, bf16[1,768,384]{2,1,0:T(8,128)(2,1)}, bf16[1,768,384]{2,1,0:T(8,128)(2,1)}, ...) | async-done | bytes 3538960 | tf_op jit(solution)/shard_map/psum | solution.py:763
  498.9 2.5 maximum_convert_fusion
  (548 shorter events, 207.1 us)
Async XLA Ops:
  7.2 411.6 %all-reduce.12.cloned.1.call-start = ((), (), s32[]{:S(2)}) async-start(), calls=%async_computation | async-start | bytes 1572864 | tf_op jit(solution)/shard_map/psum | solution.py:764
  8.6 8.5 %collective-permute-start = (bf16[8,768]{1,0:T(8,128)(2,1)}, bf16[8,768]{1,0:T(8,128)(2,1)}, u32[]{:S(2)}, u32[]{:S(2)}) collective-permute-start(bf16[8,768]{1,0:T(8,128)(2,1)} %slice.184), channel_id=1, source_target_pairs={{0,4},{4,8},{8,12},{12,16},{16,20},{20,24},{24,28},{1,5},{5,9},{9,... | collective-permute-start | bytes 36872 | tf_op jit(solution)/shard_map/ppermute | solution.py:583
  38.3 5.7 %collective-permute-start.3 = (bf16[144,384]{1,0:T(8,128)(2,1)S(1)}, bf16[144,384]{1,0:T(8,128)(2,1)S(1)}, u32[]{:S(2)}, u32[]{:S(2)}) collective-permute-start(bf16[144,384]{1,0:T(8,128)(2,1)S(1)} %get-tuple-element.127.refs_1_), channel_id=1, source_target_pairs={{0,16},{4,20},{8,24},{12,28},{16,0},{20,4},{24,8},{28,12},{1,17},{... | collective-permute-start | bytes 331784 | tf_op jit(solution)/shard_map/ppermute | solution.py:578
  48.0 6.0 %collective-permute-start.4 = (bf16[64,896]{1,0:T(8,128)(2,1)S(1)}, bf16[64,896]{1,0:T(8,128)(2,1)S(1)}, u32[]{:S(2)}, u32[]{:S(2)}) collective-permute-start(bf16[64,896]{1,0:T(8,128)(2,1)S(1)} %get-tuple-element.135), channel_id=1, source_target_pairs={{0,1},{1,0},{2,3},{3,2},{4,5},{5,4},{6,7},{7,6},{8,9},{9,8},{10,11... | collective-permute-start | bytes 344072 | tf_op jit(solution)/shard_map/ppermute | solution.py:578
  49.5 11.1 %collective-permute-start.5 = (bf16[64,896]{1,0:T(8,128)(2,1)S(1)}, bf16[64,896]{1,0:T(8,128)(2,1)S(1)}, u32[]{:S(2)}, u32[]{:S(2)}) collective-permute-start(bf16[64,896]{1,0:T(8,128)(2,1)S(1)} %get-tuple-element.136), channel_id=1, source_target_pairs={{0,2},{1,3},{2,0},{3,1},{4,6},{5,7},{6,4},{7,5},{8,10},{9,11},{10,... | collective-permute-start | bytes 344072 | tf_op jit(solution)/shard_map/ppermute | solution.py:578
  52.1 8.5 %collective-permute-start.6 = (bf16[64,896]{1,0:T(8,128)(2,1)S(1)}, bf16[64,896]{1,0:T(8,128)(2,1)S(1)}, u32[]{:S(2)}, u32[]{:S(2)}) collective-permute-start(bf16[64,896]{1,0:T(8,128)(2,1)S(1)} %get-tuple-element.137), channel_id=1, source_target_pairs={{0,3},{1,2},{2,1},{3,0},{4,7},{5,6},{6,5},{7,4},{8,11},{9,10},{10,... | collective-permute-start | bytes 344072 | tf_op jit(solution)/shard_map/ppermute | solution.py:578
  62.8 7.6 %collective-permute-start.9 = (bf16[64,896]{1,0:T(8,128)(2,1)S(1)}, bf16[64,896]{1,0:T(8,128)(2,1)S(1)}, u32[]{:S(2)}, u32[]{:S(2)}) collective-permute-start(bf16[64,896]{1,0:T(8,128)(2,1)S(1)} %get-tuple-element.138.refs_1_), channel_id=1, source_target_pairs={{0,1},{1,0},{2,3},{3,2},{4,5},{5,4},{6,7},{7,6},{8,9},{9,8},{10,11... | collective-permute-start | bytes 344072 | tf_op jit(solution)/shard_map/ppermute | solution.py:578
  64.6 10.3 %collective-permute-start.8 = (bf16[64,896]{1,0:T(8,128)(2,1)S(1)}, bf16[64,896]{1,0:T(8,128)(2,1)S(1)}, u32[]{:S(2)}, u32[]{:S(2)}) collective-permute-start(bf16[64,896]{1,0:T(8,128)(2,1)S(1)} %get-tuple-element.138.refs_1_), channel_id=1, source_target_pairs={{0,2},{1,3},{2,0},{3,1},{4,6},{5,7},{6,4},{7,5},{8,10},{9,11},{10,... | collective-permute-start | bytes 344072 | tf_op jit(solution)/shard_map/ppermute | solution.py:578
  65.9 9.0 %collective-permute-start.7 = (bf16[64,896]{1,0:T(8,128)(2,1)S(1)}, bf16[64,896]{1,0:T(8,128)(2,1)S(1)}, u32[]{:S(2)}, u32[]{:S(2)}) collective-permute-start(bf16[64,896]{1,0:T(8,128)(2,1)S(1)} %get-tuple-element.138.refs_1_), channel_id=1, source_target_pairs={{0,3},{1,2},{2,1},{3,0},{4,7},{5,6},{6,5},{7,4},{8,11},{9,10},{10,... | collective-permute-start | bytes 344072 | tf_op jit(solution)/shard_map/ppermute | solution.py:578
  122.7 19.3 %collective-permute-start.25 = (bf16[144,384]{1,0:T(8,128)(2,1)}, bf16[144,384]{1,0:T(8,128)(2,1)}, u32[]{:S(2)}, u32[]{:S(2)}) collective-permute-start(bf16[144,384]{1,0:T(8,128)(2,1)} %get-tuple-element.165.refs_1_), channel_id=1, source_target_pairs={{0,16},{4,20},{8,24},{12,28},{16,0},{20,4},{24,8},{28,12},{1,17},{... | collective-permute-start | bytes 331784 | tf_op jit(solution)/shard_map/ppermute | solution.py:578
  124.4 30.5 %collective-permute-start.14 = (bf16[64,896]{1,0:T(8,128)(2,1)}, bf16[64,896]{1,0:T(8,128)(2,1)}, u32[]{:S(2)}, u32[]{:S(2)}) collective-permute-start(bf16[64,896]{1,0:T(8,128)(2,1)} %copy-done.179), channel_id=1, source_target_pairs={{0,1},{1,0},{2,3},{3,2},{4,5},{5,4},{6,7},{7,6},{8,9},{9,8},{10,11... | collective-permute-start | bytes 344072 | tf_op jit(solution)/shard_map/ppermute | solution.py:578
  125.4 31.1 %collective-permute-start.15 = (bf16[64,896]{1,0:T(8,128)(2,1)}, bf16[64,896]{1,0:T(8,128)(2,1)}, u32[]{:S(2)}, u32[]{:S(2)}) collective-permute-start(bf16[64,896]{1,0:T(8,128)(2,1)} %copy-done.178), channel_id=1, source_target_pairs={{0,2},{1,3},{2,0},{3,1},{4,6},{5,7},{6,4},{7,5},{8,10},{9,11},{10,... | collective-permute-start | bytes 344072 | tf_op jit(solution)/shard_map/ppermute | solution.py:578
  127.2 29.3 %collective-permute-start.16 = (bf16[64,896]{1,0:T(8,128)(2,1)}, bf16[64,896]{1,0:T(8,128)(2,1)}, u32[]{:S(2)}, u32[]{:S(2)}) collective-permute-start(bf16[64,896]{1,0:T(8,128)(2,1)} %copy-done.177), channel_id=1, source_target_pairs={{0,3},{1,2},{2,1},{3,0},{4,7},{5,6},{6,5},{7,4},{8,11},{9,10},{10,... | collective-permute-start | bytes 344072 | tf_op jit(solution)/shard_map/ppermute | solution.py:578
  152.0 8.6 %collective-permute-start.27 = (bf16[64,768]{1,0:T(8,128)(2,1)S(1)}, bf16[64,768]{1,0:T(8,128)(2,1)S(1)}, u32[]{:S(2)}, u32[]{:S(2)}) collective-permute-start(bf16[64,768]{1,0:T(8,128)(2,1)S(1)} %get-tuple-element.179), channel_id=1, source_target_pairs={{0,1},{1,0},{2,3},{3,2},{4,5},{5,4},{6,7},{7,6},{8,9},{9,8},{10,11... | collective-permute-start | bytes 294920 | tf_op jit(solution)/shard_map/ppermute | solution.py:578
  152.2 12.9 %collective-permute-start.28 = (bf16[64,768]{1,0:T(8,128)(2,1)S(1)}, bf16[64,768]{1,0:T(8,128)(2,1)S(1)}, u32[]{:S(2)}, u32[]{:S(2)}) collective-permute-start(bf16[64,768]{1,0:T(8,128)(2,1)S(1)} %get-tuple-element.180), channel_id=1, source_target_pairs={{0,2},{1,3},{2,0},{3,1},{4,6},{5,7},{6,4},{7,5},{8,10},{9,11},{10,... | collective-permute-start | bytes 294920 | tf_op jit(solution)/shard_map/ppermute | solution.py:578
  154.9 10.2 %collective-permute-start.29 = (bf16[64,768]{1,0:T(8,128)(2,1)S(1)}, bf16[64,768]{1,0:T(8,128)(2,1)S(1)}, u32[]{:S(2)}, u32[]{:S(2)}) collective-permute-start(bf16[64,768]{1,0:T(8,128)(2,1)S(1)} %get-tuple-element.181), channel_id=1, source_target_pairs={{0,3},{1,2},{2,1},{3,0},{4,7},{5,6},{6,5},{7,4},{8,11},{9,10},{10,... | collective-permute-start | bytes 294920 | tf_op jit(solution)/shard_map/ppermute | solution.py:578
  158.4 16.5 %collective-permute-start.19 = (bf16[64,768]{1,0:T(8,128)(2,1)}, bf16[64,768]{1,0:T(8,128)(2,1)S(1)}, u32[]{:S(2)}, u32[]{:S(2)}) collective-permute-start(bf16[64,768]{1,0:T(8,128)(2,1)} %stream1.1.refs_1_), channel_id=1, source_target_pairs={{0,3},{1,2},{2,1},{3,0},{4,7},{5,6},{6,5},{7,4},{8,11},{9,10},{10,... | collective-permute-start | bytes 294920 | tf_op jit(solution)/shard_map/ppermute | solution.py:578
  167.9 20.2 %collective-permute-start.32 = (bf16[64,896]{1,0:T(8,128)(2,1)}, bf16[64,896]{1,0:T(8,128)(2,1)}, u32[]{:S(2)}, u32[]{:S(2)}) collective-permute-start(bf16[64,896]{1,0:T(8,128)(2,1)} %get-tuple-element.183.refs_1_), channel_id=1, source_target_pairs={{0,3},{1,2},{2,1},{3,0},{4,7},{5,6},{6,5},{7,4},{8,11},{9,10},{10,... | collective-permute-start | bytes 344072 | tf_op jit(solution)/shard_map/ppermute | solution.py:578
  170.2 17.9 %collective-permute-start.31 = (bf16[64,896]{1,0:T(8,128)(2,1)}, bf16[64,896]{1,0:T(8,128)(2,1)}, u32[]{:S(2)}, u32[]{:S(2)}) collective-permute-start(bf16[64,896]{1,0:T(8,128)(2,1)} %get-tuple-element.183.refs_1_), channel_id=1, source_target_pairs={{0,2},{1,3},{2,0},{3,1},{4,6},{5,7},{6,4},{7,5},{8,10},{9,11},{10,... | collective-permute-start | bytes 344072 | tf_op jit(solution)/shard_map/ppermute | solution.py:578
  172.1 16.1 %collective-permute-start.30 = (bf16[64,896]{1,0:T(8,128)(2,1)}, bf16[64,896]{1,0:T(8,128)(2,1)}, u32[]{:S(2)}, u32[]{:S(2)}) collective-permute-start(bf16[64,896]{1,0:T(8,128)(2,1)} %get-tuple-element.183.refs_1_), channel_id=1, source_target_pairs={{0,1},{1,0},{2,3},{3,2},{4,5},{5,4},{6,7},{7,6},{8,9},{9,8},{10,11... | collective-permute-start | bytes 344072 | tf_op jit(solution)/shard_map/ppermute | solution.py:578
  172.3 13.0 %collective-permute-start.18 = (bf16[64,768]{1,0:T(8,128)(2,1)}, bf16[64,768]{1,0:T(8,128)(2,1)}, u32[]{:S(2)}, u32[]{:S(2)}) collective-permute-start(bf16[64,768]{1,0:T(8,128)(2,1)} %stream1.1.refs_1_), channel_id=1, source_target_pairs={{0,2},{1,3},{2,0},{3,1},{4,6},{5,7},{6,4},{7,5},{8,10},{9,11},{10,... | collective-permute-start | bytes 294920 | tf_op jit(solution)/shard_map/ppermute | solution.py:578
  175.5 9.8 %collective-permute-start.17 = (bf16[64,768]{1,0:T(8,128)(2,1)}, bf16[64,768]{1,0:T(8,128)(2,1)}, u32[]{:S(2)}, u32[]{:S(2)}) collective-permute-start(bf16[64,768]{1,0:T(8,128)(2,1)} %stream1.1.refs_1_), channel_id=1, source_target_pairs={{0,1},{1,0},{2,3},{3,2},{4,5},{5,4},{6,7},{7,6},{8,9},{9,8},{10,11... | collective-permute-start | bytes 294920 | tf_op jit(solution)/shard_map/ppermute | solution.py:578
  200.5 12.2 %collective-permute-start.33 = (bf16[144,384]{1,0:T(8,128)(2,1)}, bf16[144,384]{1,0:T(8,128)(2,1)}, u32[]{:S(2)}, u32[]{:S(2)}) collective-permute-start(bf16[144,384]{1,0:T(8,128)(2,1)} %get-tuple-element.187.refs_1_), channel_id=1, source_target_pairs={{0,4},{4,0},{8,12},{12,8},{16,20},{20,16},{24,28},{28,24},{1,5},{5... | collective-permute-start | bytes 331784 | tf_op jit(solution)/shard_map/ppermute | solution.py:578
  221.2 17.3 %collective-permute-start.35 = (bf16[144,384]{1,0:T(8,128)(2,1)}, bf16[144,384]{1,0:T(8,128)(2,1)}, u32[]{:S(2)}, u32[]{:S(2)}) collective-permute-start(bf16[144,384]{1,0:T(8,128)(2,1)} %get-tuple-element.191.refs_1_), channel_id=1, source_target_pairs={{0,16},{4,20},{8,24},{12,28},{16,0},{20,4},{24,8},{28,12},{1,17},{... | collective-permute-start | bytes 331784 | tf_op jit(solution)/shard_map/ppermute | solution.py:578
  248.6 31.6 %collective-permute-start.36 = (f32[8,640]{1,0:T(8,128)}, f32[8,640]{1,0:T(8,128)}, u32[]{:S(2)}, u32[]{:S(2)}) collective-permute-start(f32[8,640]{1,0:T(8,128)} %get-tuple-element.204), channel_id=1, source_target_pairs={{4,0},{8,4},{12,8},{16,12},{20,16},{24,20},{28,24},{5,1},{9,5},{13... | collective-permute-start | bytes 61448 | tf_op jit(solution)/shard_map/ppermute | solution.py:583
  286.8 210.2 %all-reduce.14.cloned.1.call-start = ((), (), s32[]{:S(2)}) async-start(), calls=%async_computation.1 | async-start | bytes 7077888 | tf_op jit(solution)/shard_map/psum | solution.py:763
  305.6 32.3 %collective-permute-start.37 = (bf16[64,768]{1,0:T(8,128)(2,1)S(1)}, bf16[64,768]{1,0:T(8,128)(2,1)S(1)}, u32[]{:S(2)}, u32[]{:S(2)}) collective-permute-start(bf16[64,768]{1,0:T(8,128)(2,1)S(1)} %get-tuple-element.206), channel_id=1, source_target_pairs={{0,1},{1,0},{2,3},{3,2},{4,5},{5,4},{6,7},{7,6},{8,9},{9,8},{10,11... | collective-permute-start | bytes 294920 | tf_op jit(solution)/shard_map/ppermute | solution.py:578
  305.6 32.2 %collective-permute-start.38 = (bf16[64,768]{1,0:T(8,128)(2,1)S(1)}, bf16[64,768]{1,0:T(8,128)(2,1)S(1)}, u32[]{:S(2)}, u32[]{:S(2)}) collective-permute-start(bf16[64,768]{1,0:T(8,128)(2,1)S(1)} %get-tuple-element.207), channel_id=1, source_target_pairs={{0,2},{1,3},{2,0},{3,1},{4,6},{5,7},{6,4},{7,5},{8,10},{9,11},{10,... | collective-permute-start | bytes 294920 | tf_op jit(solution)/shard_map/ppermute | solution.py:578
  308.4 29.4 %collective-permute-start.39 = (bf16[64,768]{1,0:T(8,128)(2,1)S(1)}, bf16[64,768]{1,0:T(8,128)(2,1)S(1)}, u32[]{:S(2)}, u32[]{:S(2)}) collective-permute-start(bf16[64,768]{1,0:T(8,128)(2,1)S(1)} %get-tuple-element.208), channel_id=1, source_target_pairs={{0,3},{1,2},{2,1},{3,0},{4,7},{5,6},{6,5},{7,4},{8,11},{9,10},{10,... | collective-permute-start | bytes 294920 | tf_op jit(solution)/shard_map/ppermute | solution.py:578
  376.7 7.7 %collective-permute-start.42 = (bf16[64,768]{1,0:T(8,128)(2,1)S(1)}, bf16[64,768]{1,0:T(8,128)(2,1)S(1)}, u32[]{:S(2)}, u32[]{:S(2)}) collective-permute-start(bf16[64,768]{1,0:T(8,128)(2,1)S(1)} %get-tuple-element.210.refs_1_), channel_id=1, source_target_pairs={{0,3},{1,2},{2,1},{3,0},{4,7},{5,6},{6,5},{7,4},{8,11},{9,10},{10,... | collective-permute-start | bytes 294920 | tf_op jit(solution)/shard_map/ppermute | solution.py:578
  378.4 10.8 %collective-permute-start.41 = (bf16[64,768]{1,0:T(8,128)(2,1)S(1)}, bf16[64,768]{1,0:T(8,128)(2,1)S(1)}, u32[]{:S(2)}, u32[]{:S(2)}) collective-permute-start(bf16[64,768]{1,0:T(8,128)(2,1)S(1)} %get-tuple-element.210.refs_1_), channel_id=1, source_target_pairs={{0,2},{1,3},{2,0},{3,1},{4,6},{5,7},{6,4},{7,5},{8,10},{9,11},{10,... | collective-permute-start | bytes 294920 | tf_op jit(solution)/shard_map/ppermute | solution.py:578
  380.4 8.8 %collective-permute-start.40 = (bf16[64,768]{1,0:T(8,128)(2,1)S(1)}, bf16[64,768]{1,0:T(8,128)(2,1)S(1)}, u32[]{:S(2)}, u32[]{:S(2)}) collective-permute-start(bf16[64,768]{1,0:T(8,128)(2,1)S(1)} %get-tuple-element.210.refs_1_), channel_id=1, source_target_pairs={{0,1},{1,0},{2,3},{3,2},{4,5},{5,4},{6,7},{7,6},{8,9},{9,8},{10,11... | collective-permute-start | bytes 294920 | tf_op jit(solution)/shard_map/ppermute | solution.py:578
  (203 other events, 811.5 us)
Sparse Core Ops, SparseCore 0:
  286.9 131.8 all-reduce.11
  424.0 72.8 all-reduce.13

commit v2 on v1

--- a/solution.py
+++ b/solution.py
@@ -356,8 +356,7 @@
 
 
 def k_inside_back(heads, refs):
-    (act, step, cum, flags, gm, pre, low, og, normed, lowgate,
-     dxs, dbc, wout, wz) = refs
+    act, step, cum, flags, gm, pre, dxs, dbc = refs
     t, ch = gm.shape
     r, c = iotas(t, t)
     segc = seg_col(flags)
@@ -380,8 +379,6 @@
     opening = jnp.exp(cm) * jnp.where(segc == 0.0, 1.0, 0.0)
     carried = (dy.astype(F32) * spread(opening, heads)).astype(BF)
     dbc[:, N:] = dot(low_s, keys) + dot(carried, pre[...], NT)
-    wout[...] = dot(og[...], low[...], TN).astype(BF)
-    wz[...] = dot(normed[...], lowgate[...], TN).astype(BF)
 
 
 def k_state_back(layer, heads, refs):
@@ -459,9 +456,9 @@
     )
 
 
-def k_back_fix(nh, refs):
-    s_ref, part, ret, wx, wbc = refs[:5]
-    chunks, scratch = refs[5 : 5 + nh], refs[5 + nh]
+def k_back_fix(layer, nh, refs):
+    s_ref, part, ret, wx, wbc, normed, gain = refs[:7]
+    chunks, gng, scratch = refs[7 : 7 + nh], refs[7 + nh], refs[8 + nh]
     t = part.shape[0]
     ch = wx.shape[1]
     scratch[...] = part[...].astype(BF)
@@ -472,29 +469,119 @@
     rows = chunks[0].shape[0]
     for k in range(nh):
         chunks[k][...] = scratch[at_rows(s_ref, k, rows), :]
-
-
-def k_weights(refs):
-    normed, gb, ret, lowraw, wx, wbc, wdt, scratch = refs
-    t = gb.shape[0]
-    ch = wx.shape[1]
-    scratch[...] = gb[...].astype(BF)
-    tail = gb[t - 2 * HALO :, :]
+    products = jnp.sum(scratch[...].astype(F32) * normed[...].astype(F32), axis=0, keepdims=True)
+    r, _ = iotas(8, products.shape[1])
+    gng[...] = jnp.where(r == 0, products / gain[layer : layer + 1, :], 0.0)
+
+
+def k_grads(refs):
+    (s_ref, normed, gb, ret, lowraw, small, small_g, gng, lowgate, low_g, og,
+     keep, send, pack, low) = refs
+    nm = normed[...]
+    t, cc = gb.shape
+    ch = cc - 2 * N
+    d = nm.shape[1]
+    low[...] = gb[...].astype(BF)
     fix = jnp.concatenate([jnp.zeros_like(ret[...]), ret[...]], axis=0)
-    scratch[t - 2 * HALO :, :] = (tail + fix).astype(BF)
-    nm = normed[...]
-    wx[...] = dot(nm, scratch[:, :ch], TN).astype(BF)
-    wbc[...] = dot(nm, scratch[:, ch:], TN).astype(BF)
-    wdt[...] = dot(nm, lowraw[...], TN).astype(BF)
+    low[t - 2 * HALO :, :] = (gb[t - 2 * HALO :, :] + fix).astype(BF)
+    pack[:, :cc] = dot(nm, low[...], TN)
+    pack[:, cc : cc + LANES] = dot(nm, lowraw[...], TN)
+    rows = jnp.concatenate(
+        [
+            jnp.zeros((64, cc), F32),
+            small[...],
+            jnp.concatenate([small_g[...], jnp.zeros((8, cc - ch), F32)], axis=1),
+            jnp.zeros((48, cc), F32),
+        ],
+        axis=0,
+    )
+    pack[:cc, cc : cc + LANES] = pack[:cc, cc : cc + LANES] + rows.T
+    rows = jnp.concatenate([jnp.zeros((80, d), F32), gng[...], jnp.zeros((40, d), F32)], axis=0)
+    pack[:, cc : cc + LANES] = pack[:, cc : cc + LANES] + rows.T
+    at = cc + LANES
+    pack[:, at : at + ch] = dot(nm, lowgate[...], TN)
+    pack[:, at + ch : at + 2 * ch] = dot(low_g[...], og[...], TN)
+    half = keep.shape[0]
+    keep[...] = pack[at_rows(s_ref, 0, half), :].astype(BF)
+    send[...] = pack[at_rows(s_ref, 1, half), :].astype(BF)
+
+
+def k_split(chips, refs):
+    s_ref, keep, got = refs[:3]
+    chunks, scratch = refs[3 : 3 + chips], refs[3 + chips]
+    scratch[...] = keep[...].astype(F32) + got[...].astype(F32)
+    rows = chunks[0].shape[0]
+    for k in range(chips):
+        chunks[k][...] = scratch[at_rows(s_ref, k, rows), :].astype(BF)
+
+
+def k_sum(chips, ch, refs):
+    parts, refs = refs[:chips], refs[chips:]
+    total = parts[0][...].astype(F32)
+    for p in parts[1:]:
+        total = total + p[...].astype(F32)
+    refs[0][...] = total.astype(BF)
+    if len(refs) > 1:
+        refs[1][...] = total[:, ch : ch + 2 * N + LANES].astype(BF)
+
+
+def k_head_part(nh, ch, refs):
+    share, parts, out = refs[0], refs[1 : 1 + nh], refs[1 + nh]
+    total = parts[0][...].astype(F32)
+    for p in parts[1:]:
+        total = total + p[...].astype(F32)
+    out[...] = share[...]
+    out[:, ch : ch + 2 * N] = total[:, : 2 * N].astype(BF)
+    own = share[:, ch + 2 * N : ch + 2 * N + LANES].astype(F32)
+    moved = pltpu.roll(total[:, 2 * N :], 32, axis=1)
+    _, c = iotas(own.shape[0], LANES)
+    out[:, ch + 2 * N : ch + 2 * N + LANES] = jnp.where(c >= 96, moved, own).astype(BF)
+
+
+def k_finish(chips, last, refs):
+    s_ref, mine, theirs, refs = refs[0], refs[1], refs[2], refs[3:]
+    if last:
+        other, refs = refs[3], refs[4:]
+    wzx, wbc, wo, small = refs[:4]
+    pack = refs[-1]
+    rows = mine.shape[0] // chips
+    for k in range(chips):
+        for half, src in ((0, mine), (1, theirs)):
+            pack[at_rows(s_ref, half * chips + k, rows), :] = src[
+                k * rows : (k + 1) * rows, :
+            ].astype(F32)
+    ch = wzx.shape[-1]
+    cc = ch + 2 * N
+    at = cc + LANES
+    wzx[1] = pack[:, :ch]
+    wbc[...] = pack[:, ch:cc]
+    small[...] = pack[:, cc:at].T
+    wzx[0] = pack[:, at : at + ch]
+    wo[...] = pack[:, at + ch : at + 2 * ch].T
+    if last:
+        gg, dt, cx, cxb, cbc, cbcb, gate, skip, dtb, alog = refs[4:-1]
+        heads = dtb.shape[1]
+        for l, src in ((0, small), (1, other)):
+            gg[l : l + 1, :] = src[112:113, :]
+            dt[:, l, :] = src[0:heads, :]
+            cx[l] = src[64:68, :ch]
+            cxb[l : l + 1, :] = src[68:69, :ch]
+            cbc[l] = src[96:100, ch:cc]
+            cbcb[l : l + 1, :] = src[100:101, ch:cc]
+            gate[l : l + 1, :] = src[72:73, :ch]
+            skips = head_sum(jnp.broadcast_to(src[73:74, :ch], (8, ch)))
+            skip[l : l + 1, :] = skips[0:1, :heads]
+            dtb[l : l + 1, :] = src[69:70, :heads]
+            alog[l : l + 1, :] = src[70:71, :heads]
 
 
 def k_norm_back(layer, nh, refs):
     s_ref, parts, refs = refs[0], refs[1 : 1 + nh], refs[1 + nh :]
     final = layer == LAYERS - 1
     if layer > 0:
-        r_own, g_in, gain, total, g_out, gng, pay = refs
+        r_own, g_in, gain, total, g_out, pay = refs
     else:
-        r_own, g_in, gain, gng, pay = refs
+        r_own, g_in, gain, pay = refs
     rows, d = parts[0].shape
     gn = parts[0][...].astype(F32)
     for p in parts[1:]:
@@ -505,7 +592,6 @@
     ri = r * inv
     gg = gn * gain[layer : layer + 1, :]
     new = old + inv * (gg - ri * jnp.mean(gg * ri, axis=1, keepdims=True))
-    gng[...] = jnp.broadcast_to(jnp.sum(gn * ri, axis=0, keepdims=True), (8, d))
     if layer > 0:
         g_out[...] = new
         low = new.astype(BF)
@@ -524,11 +610,43 @@
         self.array, self.lead = array, lead
 
 
-def call(body, name, args, outs, scratch=(), flops=0):
+class Whole:
+    def __init__(self, array):
+        self.array = array
+
+
+class After(Whole):
+    pass
+
+
+class Part:
+    def __init__(self, shape, dtype, *lead):
+        self.shape, self.dtype, self.lead = shape, dtype, lead
+
+
+class Loose:
+    def __init__(self, array):
+        self.array = array
+
+
+def call(body, name, args, outs, scratch=(), flops=0, loose=False, aliases=None, after=()):
+    count_in = len(args)
+    args = list(args) + [After(a) for a in after]
     specs, arrays = [], []
     size = 0
     for a in args:
-        if isinstance(a, Layered):
+        if isinstance(a, After):
+            specs.append(pl.BlockSpec(memory_space=pltpu.HBM))
+            arrays.append(pltpu.with_memory_space_constraint(a.array, pltpu.HBM))
+        elif isinstance(a, Whole):
+            specs.append(pl.BlockSpec(memory_space=pltpu.HBM))
+            arrays.append(a.array)
+        elif isinstance(a, Loose):
+            a = a.array
+            specs.append(pl.BlockSpec(a.shape, functools.partial(lambda n, i: (0,) * n, a.ndim)))
+            arrays.append(a)
+            size += a.size * a.dtype.itemsize
+        elif isinstance(a, Layered):
             rest = a.array.shape[len(a.lead) :]
             lead = a.lead
             specs.append(
@@ -537,7 +655,7 @@
                     functools.partial(lambda lead, n, i: lead + (0,) * n, lead, len(rest)),
                 )
             )
-            arrays.append(a.array)
+            arrays.append(pltpu.with_memory_space_constraint(a.array, pltpu.HBM))
             count = 1
             for s in rest:
                 count *= s
@@ -547,26 +665,46 @@
             arrays.append(a)
         else:
             specs.append(pl.BlockSpec(a.shape, functools.partial(lambda n, i: (0,) * n, a.ndim)))
-            arrays.append(a)
+            arrays.append(pltpu.with_memory_space_constraint(a, pltpu.HBM))
             size += a.size * a.dtype.itemsize
-    for s, t in outs:
+    out_specs, out_shapes = [], []
+    for o in outs:
+        if isinstance(o, Part):
+            rest = o.shape[len(o.lead) :]
+            out_specs.append(
+                pl.BlockSpec(
+                    (None,) * len(o.lead) + rest,
+                    functools.partial(lambda lead, n, i: lead + (0,) * n, o.lead, len(rest)),
+                )
+            )
+            shape, dtype = o.shape, o.dtype
+            out_shapes.append(pltpu.HBM(shape, dtype))
+        else:
+            shape, dtype = o[0], o[1]
+            rest = shape
+            out_specs.append(
+                pl.BlockSpec(shape, functools.partial(lambda n, i: (0,) * n, len(shape)))
+            )
+            free = loose or len(o) > 2
+            out_shapes.append(
+                jax.ShapeDtypeStruct(shape, dtype) if free else pltpu.HBM(shape, dtype)
+            )
         count = 1
-        for k in s:
+        for k in rest:
             count *= k
-        size += count * jnp.dtype(t).itemsize
+        size += count * jnp.dtype(dtype).itemsize
 
     def kernel(*refs):
-        body(refs)
+        body(refs[:count_in] + refs[count_in + len(after) :])
 
     return pl.pallas_call(
         kernel,
-        out_shape=[jax.ShapeDtypeStruct(s, t) for s, t in outs],
+        out_shape=out_shapes,
         grid=(1,),
         in_specs=specs,
-        out_specs=[
-            pl.BlockSpec(s, functools.partial(lambda n, i: (0,) * n, len(s))) for s, _ in outs
-        ],
+        out_specs=out_specs,
         scratch_shapes=[pltpu.VMEM(s, t) for s, t in scratch],
+        input_output_aliases=aliases or {},
         compiler_params=pltpu.CompilerParams(vmem_limit_bytes=48 << 20),
         cost_estimate=pl.CostEstimate(flops=flops, bytes_accessed=size, transcendentals=0),
         name=name,
@@ -597,9 +735,9 @@
         outs = [((N, ch), out_type if last else F32)]
         if not last:
             outs += [((8, ch), F32), ((N + TH, ch), BF)]
-        args = [flag, pay, got] + ([] if first else [pre, q])
+        args = [flag, Loose(pay), Loose(got)] + ([] if first else [Loose(pre), Loose(q)])
         res = call(
-            functools.partial(k_combine, first, last), "combine", args, outs
+            functools.partial(k_combine, first, last), "combine", args, outs, loose=True
         )
         pre = res[0]
         if not last:
@@ -610,12 +748,12 @@
 
 def to_shares(chunks):
     nh = lax.axis_size("head")
-    return [chunks[0]] + [swap(chunks[k], "head", k) for k in range(1, nh)]
+    return [Loose(chunks[0])] + [Loose(swap(chunks[k], "head", k)) for k in range(1, nh)]
 
 
 def from_shares(share):
     nh = lax.axis_size("head")
-    return [share] + [swap(share, "head", k) for k in range(1, nh)]
+    return [Loose(share)] + [Loose(swap(share, "head", k)) for k in range(1, nh)]
 
 
 def layer_forward(layer, src, halo_raw, prm, flags, order, width, cot):
@@ -637,10 +775,10 @@
         )
         invc = None
     else:
-        rows = src[0].shape[0]
+        rows = src[0].array.shape[0]
         tail = jnp.zeros((HALO, d), BF)
         for k in range(nh):
-            tail = jnp.where(order[k] == nh - 1, src[k][rows - HALO :, :d], tail)
+            tail = jnp.where(order[k] == nh - 1, src[k].array[rows - HALO :, :d], tail)
         halo = passed(tail, "seq", 1)
         gate, cin, dtr, normed, invc = call(
             functools.partial(k_project, layer, nh), "project1",
@@ -648,9 +786,9 @@
         )
     act, ds, hc, step, cum, pay = call(
         functools.partial(k_conv, layer, heads, layer == 0), "conv",
-        [halo, norm_gain, cin, dtr, flags, wx, wbc, cx, cxb, cbc, cbcb, dtb, alog],
+        [Loose(halo), norm_gain, cin, dtr, flags, wx, wbc, cx, cxb, cbc, cbcb, dtb, alog],
         [((t, cc), BF), ((t, cc), BF), ((HALO, cc), BF), ((t, LANES), F32), ((t, LANES), F32),
-         ((N + TH, ch), BF)],
+         ((N + TH, ch), BF, 1)],
         [((t + HALO, cc), F32)],
         flops=2 * t * N * ch,
     )
@@ -661,11 +799,11 @@
     )
     final = layer == LAYERS - 1
     rows = t // nh
-    outs = [((t, ch), F32)] + [((rows, d + LANES), BF)] * nh
-    args = [order, pre, act, cum, flags, yin, gate, gate_gain, skip, wo]
+    outs = [((t, ch), F32)] + [((rows, d + LANES), BF, 1)] * nh
+    args = [order, Loose(pre), act, cum, flags, yin, gate, gate_gain, skip, wo]
     if final:
         args.append(cot)
-        outs += [((t, ch), F32), ((8, t), F32)]
+        outs += [((t, ch), F32), ((8, t), F32, 1)]
     res = call(
         functools.partial(k_output, layer, heads, nh), "output", args, outs,
         [((t, d + LANES), BF)], flops=2 * t * ch * d,
@@ -679,7 +817,7 @@
     return res[1 : 1 + nh], invc, stored
 
 
-def layer_backward(layer, sv, low_src, invc, prm, flags, order, width, own):
+def layer_backward(layer, sv, low_src, invc, prm, flags, order, width, own, before):
     nh = lax.axis_size("head")
     norm_gain, in_zx, in_bc, in_dt, dtb, alog, skip, cx, cxb, cbc, cbcb, gate_gain, out_proj = prm
     d, ch = in_zx.shape[2], in_zx.shape[3]
@@ -689,7 +827,7 @@
     rows = t // nh
     wz, wx = Layered(in_zx, layer, 0), Layered(in_zx, layer, 1)
     wbc, wdt, wo = Layered(in_bc, layer), Layered(in_dt, layer), Layered(out_proj, layer)
-    outs = [((N + TH, ch), BF), ((t, ch), BF), ((t, ch), BF), ((t, ch), BF), ((8, ch), F32)]
+    outs = [((N + TH, ch), BF, 1), ((t, ch), BF), ((t, ch), BF), ((t, ch), BF), ((8, ch), F32)]
     common = [gate_gain, sv["y0"], sv["gate"], sv["act"], sv["cum"], flags, skip]
     body = functools.partial(k_gate_back, layer, heads, nh)
     if layer == LAYERS - 1:
@@ -702,94 +840,84 @@
         pay, gm, lowgate, og, small_g, low = call(
             body, "gateback0",
             [order, *low_src, wo, invc, width, *common], outs + [((t, d), BF)],
-            [((t, LANES), F32)], flops=2 * t * ch * d,
+            [((t, LANES), F32)], flops=2 * t * ch * d, after=before["gate"],
         )
     state_grad = scan_blocks(pay, False, F32)
-    dxs, dbc, w_out, w_z = call(
+    dxs, dbc = call(
         functools.partial(k_inside_back, heads), "insideback",
-        [sv["act"], sv["step"], sv["cum"], flags, gm, sv["pre"], low, og, sv["normed"], lowgate],
-        [((t, ch), F32), ((t, 2 * N), F32), ((ch, d), BF), ((d, ch), BF)],
-        flops=2 * t * t * ch * 4 + 4 * t * d * ch,
+        [sv["act"], sv["step"], sv["cum"], flags, gm, sv["pre"]],
+        [((t, ch), F32), ((t, 2 * N), F32)],
+        flops=2 * t * t * ch * 4, after=before["inside"],
     )
     gb, gh, lowraw, small = call(
         functools.partial(k_state_back, layer, heads), "stateback",
-        [state_grad, sv["pre"], sv["act"], sv["step"], sv["cum"], sv["dtr"], flags, gm, sv["y0"],
+        [Loose(state_grad), sv["pre"], sv["act"], sv["step"], sv["cum"], sv["dtr"], flags, gm, sv["y0"],
          dxs, dbc, sv["ds"], sv["cin"], sv["hc"], cx, cbc, skip, dtb, alog],
-        [((t, cc), F32), ((HALO, cc), F32), ((t, LANES), BF), ((8, cc), F32)],
+        [((t, cc), F32), ((HALO, cc), F32, 1), ((t, LANES), BF), ((8, cc), F32)],
         [((t + HALO, cc), F32), ((t + 2 * HALO, cc), F32)],
-        flops=4 * t * N * ch,
+        flops=4 * t * N * ch, after=before["state"],
     )
     ret = passed(gh, "seq", -1)
     (part,) = call(
         k_back_project, "backproject", [lowgate, gb, lowraw, wz, wx, wbc, wdt], [((t, d), F32)],
-        flops=2 * t * d * (2 * ch + 3 * N),
-    )
-    chunks = call(
-        functools.partial(k_back_fix, nh), "backfix", [order, part, ret, wx, wbc],
-        [((rows, d), BF)] * nh, [((t, d), BF)], flops=2 * 2 * HALO * d * cc,
+        flops=2 * t * d * (2 * ch + 3 * N), after=before["project"],
+    )
+    *chunks, gng = call(
+        functools.partial(k_back_fix, layer, nh), "backfix",
+        [order, part, Loose(ret), wx, wbc, sv["normed"], norm_gain],
+        [((rows, d), BF, 1)] * nh + [((8, d), F32)], [((t, d), BF)], flops=2 * 2 * HALO * d * cc,
+        after=before["fix"],
     )
     parts = to_shares(chunks)
-    w_x, w_bc, w_dt = call(
-        k_weights, "weights", [sv["normed"], gb, ret, lowraw],
-        [((d, ch), BF), ((d, 2 * N), BF), ((d, LANES), BF)], [((t, cc), BF)],
-        flops=2 * t * d * (ch + 3 * N),
-    )
     body = functools.partial(k_norm_back, layer, nh)
     if layer > 0:
         r_own, g_in, total = own
-        g_own, gng, share = call(
+        g_own, share = call(
             body, "normback1", [order, *parts, r_own, g_in, norm_gain, total],
-            [((rows, d), F32), ((8, d), F32), ((rows, d + LANES), BF)],
+            [((rows, d), F32), ((rows, d + LANES), BF, 1)],
         )
     else:
         r_own, g_in = own
-        gng, share = call(
-            body, "normback0", [order, *parts, r_own, g_in, norm_gain],
-            [((8, d), F32), ((rows, d), BF)],
+        (share,) = call(
+            body, "normback0", [order, *parts, r_own, g_in, norm_gain], [((rows, d), BF)],
         )
         g_own = None
-    grads = dict(
-        w_out=w_out, w_z=w_z, w_x=w_x, w_bc=w_bc, w_dt=w_dt, small=small, small_g=small_g,
-        gng=gng[0],
-    )
-    return from_shares(share), g_own, grads
-
-
-def summed(grads, heads):
-    small, small_g = grads["small"], grads["small_g"]
-    ch = small_g.shape[1]
-    g_skip = jnp.sum(small_g[1].reshape(heads, P_SIZE), axis=1)
-    over_seq = [grads["w_z"], grads["w_x"], grads["w_dt"][:, :heads], grads["w_out"]]
-    over_seq = [lax.psum(a, "seq").astype(F32) for a in over_seq]
-    w_bc = lax.psum(grads["w_bc"], ("seq", "head")).astype(F32)
-    flat = lax.psum(
-        jnp.concatenate(
-            [small[:5, :ch].reshape(-1), small_g[0], g_skip, small[5, :heads], small[6, :heads]]
-        ),
-        "seq",
-    )
-    both = lax.psum(
-        jnp.concatenate([small[:5, ch:].reshape(-1), grads["gng"]]), ("seq", "head")
-    )
-    w_z, w_x, w_dt, w_out = over_seq
-    x_rows = flat[: 5 * ch].reshape(5, ch)
-    rest = flat[5 * ch :]
-    bc = both[: 5 * 2 * N].reshape(5, 2 * N)
-    return (
-        both[5 * 2 * N :],
-        jnp.stack([w_z, w_x]),
-        w_bc,
-        w_dt,
-        rest[ch + heads : ch + 2 * heads],
-        rest[ch + 2 * heads : ch + 3 * heads],
-        rest[ch : ch + heads],
-        x_rows[:4],
-        x_rows[4],
-        bc[:4],
-        bc[4],
-        rest[:ch],
-        w_out,
-    )
+    late = [sv["normed"], gb, Loose(ret), lowraw, small, small_g, gng, lowgate, low, og]
+    return from_shares(share), g_own, late, dict(inside=dxs, fix=gng, share=share)
+
+
+def reduced(grads, ch, before):
+    count, nh = lax.axis_size("seq"), lax.axis_size("head")
+    chips = count // 2
+    place = lax.axis_index("seq")
+    core, chip = place % 2, place // 2
+    sides = jnp.stack([core, 1 - core]).astype(jnp.int32)
+    near = (chip ^ jnp.arange(chips, dtype=jnp.int32)).astype(jnp.int32)
+    t, d = grads[0].shape
+    wide = 3 * ch + 2 * N + LANES
+    half, rows = d // 2, d // count
+    keep, send = call(
+        k_grads, "grads", [sides, *grads], [((half, wide), BF)] * 2,
+        [((d, wide), F32), ((t, ch + 2 * N), BF)], flops=2 * t * d * wide, after=before["grads"],
+    )
+    got = swap(send, "seq", 1)
+    chunks = call(
+        functools.partial(k_split, chips), "split", [near, keep, Loose(got)],
+        [((rows, wide), BF)] * chips, [((half, wide), F32)],
+    )
+    parts = [chunks[0]] + [Loose(swap(chunks[k], "seq", 2 * k)) for k in range(1, chips)]
+    summed, heads_part = call(
+        functools.partial(k_sum, chips, ch), "sum", parts,
+        [((rows, wide), BF), ((rows, 2 * N + LANES), BF, 1)], after=before["sum"],
+    )
+    (share,) = call(
+        functools.partial(k_head_part, nh, ch), "headpart", [summed, *from_shares(heads_part)],
+        [((rows, wide), BF)], after=before["head"],
+    )
+    mine = jnp.concatenate([share] + [swap(share, "seq", 2 * k) for k in range(1, chips)], axis=0)
+    theirs = swap(mine, "seq", 1)
+    order = jnp.concatenate([core * chips + near, (1 - core) * chips + near]).astype(jnp.int32)
+    return [order, Loose(mine), Loose(theirs)], dict(split=chunks[0], sum=summed, head=share)
 
 
 def per_device(
@@ -818,30 +946,58 @@
     r1, total0, share = call(
         functools.partial(k_stream, 0, nh), "stream0",
         [order, *to_shares(chunks), stream, norm_gain, width],
-        [((rows, d), F32), ((rows, d), F32), ((rows, d + LANES), BF)],
+        [((rows, d), F32), ((rows, d), F32), ((rows, d + LANES), BF, 1)],
     )
     chunks, invc0, sv1 = layer_forward(
         1, from_shares(share), None, prm, flags, order, width, cotangent
     )
-    low, g1, grads1 = layer_backward(
-        1, sv1, cotangent, None, prm, flags, order, width, (r1, cotangent, total0)
-    )
+    none = dict(gate=[], inside=[], state=[], project=[], fix=[])
+    low, g1, grads1, _ = layer_backward(
+        1, sv1, cotangent, None, prm, flags, order, width, (r1, cotangent, total0), none
+    )
+    held = dict(grads=[], sum=[], head=[])
+    pieces1, marks = reduced(grads1, ch, held)
+    before = dict(none, gate=[marks["split"]], inside=[marks["sum"]])
+    last, _, grads0, done = layer_backward(
+        0, sv0, low, invc0, prm, flags, order, width, (stream, g1), before
+    )
+    (grad_stream,) = call(
+        functools.partial(k_join, nh), "join", [order, *last], [((t, d), F32)]
+    )
+    pieces0, marks = reduced(grads0, ch, dict(grads=[], sum=[done["share"]], head=[]))
     (out_share,) = call(
         functools.partial(k_stream_last, nh), "stream1",
-        [order, *to_shares(chunks), r1, width], [((rows, d), BF)],
+        [order, *to_shares(chunks), r1, width], [((rows, d), BF, 1)],
     )
     (output,) = call(
         functools.partial(k_join, nh), "join", [order, *from_shares(out_share)], [((t, d), F32)]
     )
-    last, _, grads0 = layer_backward(
-        0, sv0, low, invc0, prm, flags, order, width, (stream, g1)
-    )
-    (grad_stream,) = call(
-        functools.partial(k_join, nh), "join", [order, *last], [((t, d), F32)]
-    )
-    per_layer = [summed(grads0, heads), summed(grads1, heads)]
-    stacked = [jnp.stack(pair) for pair in zip(*per_layer)]
-    return (output, grad_stream, *stacked)
+    chips = lax.axis_size("seq") // 2
+    wide = 3 * ch + 2 * N + LANES
+    scratch = [((d, wide), F32)]
+
+    def outs(layer):
+        return [
+            Part(in_zx.shape, F32, layer), Part(in_bc.shape, F32, layer),
+            Part(out_proj.shape, F32, layer), ((LANES, d), F32),
+        ]
+
+    g_zx, g_bc, g_wo, small1 = call(
+        functools.partial(k_finish, chips, False), "finish1", pieces1, outs(1), scratch
+    )
+    tiny = [
+        (LAYERS, d), (heads, LAYERS, d), conv_x.shape, conv_x_bias.shape, conv_bc.shape,
+        conv_bc_bias.shape, gate_gain.shape, skip_d.shape, dt_bias.shape, a_log.shape,
+    ]
+    g_zx, g_bc, g_wo, _, gg, g_dt, cx, cxb, cbc, cbcb, gate, g_skip, g_dtb, g_alog = call(
+        functools.partial(k_finish, chips, True), "finish0",
+        [*pieces0, Whole(g_zx), Whole(g_bc), Whole(g_wo), small1],
+        outs(0) + [(shape, F32) for shape in tiny], scratch, aliases={3: 0, 4: 1, 5: 2},
+    )
+    return (
+        output, grad_stream, gg, g_zx, g_bc, jnp.transpose(g_dt, (1, 2, 0)), g_dtb, g_alog,
+        g_skip, cx, cxb, cbc, cbcb, gate, g_wo,
+    )
 
 
 def solution(mesh):

time: 513 us -> 306 us (0.60)
  local copies, waits for them, and re-layouts: 109 us -> 6.4 us
  blocking collectives: 91.2 us -> 0 us
  waiting for transfers between devices: 157 us -> 102 us
  Pallas kernels: 54.3 us -> 103 us
  starting transfers between devices: 61 us -> 84.8 us
  other arithmetic: 18.9 us -> 0.33 us
  between operations: 18.2 us -> 3.97 us
    psum x2 -> x0, waiting for transfers between devices: 104 us -> none  [the longest x1 75.8 us: summed(): over_seq = [lax.psum(a, 'seq').astype(F32) for a in over_seq]]
    psum x3 -> x0, blocking collectives: 91.2 us -> none  [the longest x1 38 us: summed(): lax.psum(jnp.concatenate([small[:5, ch:].reshape(-1), grads['gng']]), ('s...]
    unnamed x381 -> x27, local copies, waits for them, and re-layouts: 83.4 us -> 2.57 us
    ppermute x39 -> x61, waiting for transfers between devices: 52.2 us -> 102 us  [swap(): return lax.ppermute(array, axis, [(i, i ^ by) for i in range(count)])]
    pallas_call x38 -> x46, Pallas kernels: 54.3 us -> 103 us  [call(): pl.pallas_call(kernel, out_shape=out_shapes, grid=(1,), in_specs=specs, o...]
    ppermute x39 -> x61, starting transfers between devices: 53.8 us -> 78 us  [swap(): return lax.ppermute(array, axis, [(i, i ^ by) for i in range(count)])]
    another operation x14 -> x1, other arithmetic: 16.3 us -> 0.07 us  [reduced(): sides = jnp.stack([core, 1 - core]).astype(jnp.int32)]
    slice x22 -> x1, local copies, waits for them, and re-layouts: 9.97 us -> 0.59 us  [layer_forward(): tail = jnp.where(order[k] == nh - 1, src[k].array[rows - HALO:, :d], tail)]
  transfers between devices with their start and end apart: 45 -> 65, of which waited for: 21 -> 32; matrix products, arithmetic and copies ran while one was open for 7% -> 1% of each run, Pallas kernels for 5% -> 17%
where the time goes in v2:
time: 306 us; the launch traced here: 300 us
  Pallas kernels  103 us (34%)
  waiting for transfers between devices  102 us (33%)
  starting transfers between devices  84.8 us (28%)
  local copies, waits for them, and re-layouts  6.4 us (2%)
  between operations  3.97 us (1%)
    pallas_call x46, Pallas kernels, call(): pl.pallas_call(kernel, out_shape=out_shapes, grid=(1,), in_specs=specs, o...  103 us
    ppermute x61, waiting for transfers between devices, swap(): return lax.ppermute(array, axis, [(i, i ^ by) for i in range(count)])  102 us
    ppermute x61, starting transfers between devices, swap(): return lax.ppermute(array, axis, [(i, i ^ by) for i in range(count)])  78 us
    ppermute x4, starting transfers between devices, passed(): lax.ppermute(array, axis, [(i, i + by) for i in range(count) if 0 <= i +...  6.87 us
  transfers between devices with their start and end apart: 65, of which 32 were waited for; matrix products, arithmetic and copies ran while one was open for 1% of the time, Pallas kernels for 17%

profile of v2, /device:TPU:0, one launch (start us, length us, event | category | flops | bytes accessed | tf_op | source)
XLA Modules:
  0.0 300.3 jit_solution(7428344496665748496)
XLA Ops:
  5.6 3.2 %project0.1 = (f32[256,384]{1,0:T(8,128)}, bf16[256,640]{1,0:T(8,128)(2,1)}, f32[256,128]{1,0:T(8,128)}, bf16[256,768]{1,0:T(8,128)(2,1)}) custom-call(bf16[256,768]{1,0:T(8,128)(2,1)} %refs_5_.15, f32[2,768]{1,0:T(2,128)} %refs_7_.13, bf16[2,2,768,384]{3,2,1,0:T(8,128)(2,1)} %refs_3_.9, bf16[2,2,768,384]{3,2,1,0:T(8,128)(2,1)} %refs_3_.9, ...), custom_call_target="tpu_custom_call" | custom-call | flops 452984832 | bytes 3414016 | tf_op jit(solution)/shard_map/project0/pallas_call | solution.py:700
  9.9 3.4 %conv.2 = (bf16[256,640]{1,0:T(8,128)(2,1)}, bf16[256,640]{1,0:T(8,128)(2,1)}, bf16[8,640]{1,0:T(8,128)(2,1)}, f32[256,128]{1,0:T(8,128)}, f32[256,128]{1,0:T(8,128)}, /*index=5*/bf16[144,384]{1,0:T(8,128)(2,1)S(1)}) custom-call(bf16[8,768]{1,0:T(8,128)(2,1)S(1)} %collective-permute-done.refs_0_, f32[2,768]{1,0:T(2,128)} %refs_7_.13, ...), custom_call_target="tpu_custom_call" | custom-call | flops 25165824 | bytes 2527232 | tf_op jit(solution)/shard_map/conv/pallas_call | solution.py:700
  19.1 3.3 %collective-permute-done.2.refs_2_ = bf16[144,384]{1,0:T(8,128)(2,1)S(1)} collective-permute-done((bf16[144,384]{1,0:T(8,128)(2,1)S(1)}, bf16[144,384]{1,0:T(8,128)(2,1)S(1)}, u32[]{:S(2)}, u32[]{:S(2)}) %collective-permute-start.2) | collective-permute-done | bytes 110624 | tf_op jit(solution)/shard_map/ppermute | solution.py:716
  24.0 3.1 %inside.2.refs_5_ = f32[256,384]{1,0:T(8,128)} custom-call(bf16[256,640]{1,0:T(8,128)(2,1)} %get-tuple-element.152.refs_0_.refs_2_.refs_11_, f32[256,128]{1,0:T(8,128)} %get-tuple-element.154.refs_1_.refs_3_, f32[256,128]{1,0:T(8,128)} %get-tuple-element.153.refs_2_.refs_3_.refs_12_.refs_4_, s32[1,256]{1,0:T(1,128)} %bitcast.13), custom_call_target="tpu_custom_call" | custom-call | flops 100663296 | bytes 984064 | tf_op jit(solution)/shard_map/inside/pallas_call | solution.py:700
  36.2 6.5 %collective-permute-done.5.refs_3_ = bf16[64,896]{1,0:T(8,128)(2,1)S(1)} collective-permute-done((bf16[64,896]{1,0:T(8,128)(2,1)S(1)}, bf16[64,896]{1,0:T(8,128)(2,1)S(1)}, u32[]{:S(2)}, u32[]{:S(2)}) %collective-permute-start.5) | collective-permute-done | bytes 114720 | tf_op jit(solution)/shard_map/ppermute | solution.py:716
  52.5 3.2 %collective-permute-done.8.refs_3_ = bf16[64,896]{1,0:T(8,128)(2,1)S(1)} collective-permute-done((bf16[64,896]{1,0:T(8,128)(2,1)S(1)}, bf16[64,896]{1,0:T(8,128)(2,1)S(1)}, u32[]{:S(2)}, u32[]{:S(2)}) %collective-permute-start.8) | collective-permute-done | bytes 114720 | tf_op jit(solution)/shard_map/ppermute | solution.py:716
  60.2 3.3 %conv.3 = (bf16[256,640]{1,0:T(8,128)(2,1)}, bf16[256,640]{1,0:T(8,128)(2,1)}, bf16[8,640]{1,0:T(8,128)(2,1)}, f32[256,128]{1,0:T(8,128)}, f32[256,128]{1,0:T(8,128)}, /*index=5*/bf16[144,384]{1,0:T(8,128)(2,1)S(1)}) custom-call(bf16[8,768]{1,0:T(8,128)(2,1)S(1)} %collective-permute-done.10.refs_0_, f32[2,768]{1,0:T(2,128)} %refs_7_.13, ...), custom_call_target="tpu_custom_call" | custom-call | flops 25165824 | bytes 2527232 | tf_op jit(solution)/shard_map/conv/pallas_call | solution.py:700
  67.7 3.8 %collective-permute-done.12.refs_2_ = bf16[144,384]{1,0:T(8,128)(2,1)S(1)} collective-permute-done((bf16[144,384]{1,0:T(8,128)(2,1)S(1)}, bf16[144,384]{1,0:T(8,128)(2,1)S(1)}, u32[]{:S(2)}, u32[]{:S(2)}) %collective-permute-start.12) | collective-permute-done | bytes 110624 | tf_op jit(solution)/shard_map/ppermute | solution.py:716
  76.5 3.6 %output.3 = (f32[256,384]{1,0:T(8,128)}, bf16[64,896]{1,0:T(8,128)(2,1)S(1)}, bf16[64,896]{1,0:T(8,128)(2,1)}, bf16[64,896]{1,0:T(8,128)(2,1)}, bf16[64,896]{1,0...) custom-call(s32[4]{0:T(128)S(1)} %iota_xor_fusion.1.refs_0_, bf16[128,384]{1,0:T(8,128)(2,1)S(1)} %combine.17.refs_1_.refs_5_, ...), custom_call_target="tpu_custom_call" | custom-call | flops 150994944 | bytes 3585024 | tf_op jit(solution)/shard_map/output/pallas_call | solution.py:700
  85.3 3.6 %collective-permute-done.22.refs_3_ = f32[8,256]{1,0:T(8,128)S(1)} collective-permute-done((f32[8,256]{1,0:T(8,128)S(1)}, f32[8,256]{1,0:T(8,128)S(1)}, u32[]{:S(2)}, u32[]{:S(2)}) %collective-permute-start.22) | collective-permute-done | bytes 8224 | tf_op jit(solution)/shard_map/ppermute | solution.py:716
  94.6 3.6 %collective-permute-done.24.refs_2_ = bf16[144,384]{1,0:T(8,128)(2,1)S(1)} collective-permute-done((bf16[144,384]{1,0:T(8,128)(2,1)S(1)}, bf16[144,384]{1,0:T(8,128)(2,1)S(1)}, u32[]{:S(2)}, u32[]{:S(2)}) %collective-permute-start.24) | collective-permute-done | bytes 110624 | tf_op jit(solution)/shard_map/ppermute | solution.py:716
  99.6 4.6 %insideback.2 = (f32[256,384]{1,0:T(8,128)}, f32[256,256]{1,0:T(8,128)}) custom-call(bf16[256,640]{1,0:T(8,128)(2,1)} %get-tuple-element.170.refs_0_.refs_2_.refs_9_, f32[256,128]{1,0:T(8,128)} %get-tuple-element.172.refs_1_.refs_3_, f32[256,128]{1,0:T(8,128)} %get-tuple-element.171.refs_2_.refs_3_.refs_10_.refs_4_, s32[1,256]{1,0:T(1,128)} %bitcast.19, ...), custom_call_target="tpu_custom_call" | custom-call | flops 201326592 | bytes 1541120 | tf_op jit(solution)/shard_map/insideback/pallas_call | solution.py:700
  104.2 5.8 %stateback.2 = (f32[256,640]{1,0:T(8,128)}, f32[8,640]{1,0:T(8,128)S(1)}, bf16[256,128]{1,0:T(8,128)(2,1)}, f32[8,640]{1,0:T(8,128)}) custom-call(f32[128,384]{1,0:T(8,128)S(1)} %combine.20.refs_0_, bf16[128,384]{1,0:T(8,128)(2,1)} %copy-done, bf16[256,640]{1,0:T(8,128)(2,1)} %get-tuple-element.170.refs_0_.refs_2_.refs_9_, ...), custom_call_target="tpu_custom_call" | custom-call | flops 50331648 | bytes 3713024 | tf_op jit(solution)/shard_map/stateback/pallas_call | solution.py:700
  111.6 3.4 %backproject.2.refs_1_ = f32[256,768]{1,0:T(8,128)} custom-call(bf16[256,384]{1,0:T(8,128)(2,1)} %get-tuple-element.182.refs_0_.refs_8_, f32[256,640]{1,0:T(8,128)} %get-tuple-element.195.refs_1_.refs_2_, bf16[256,128]{1,0:T(8,128)(2,1)} %get-tuple-element.196.refs_2_.refs_4_, bf16[2,2,768,384]{3,2,1,0:T(8,128)(2,1)} %refs_3_.9, ...), custom_call_target="tpu_custom_call" | custom-call | flops 452984832 | bytes 3473408 | tf_op jit(solution)/shard_map/backproject/pallas_call | solution.py:700
  117.5 4.0 %grads.2 = (bf16[384,1536]{1,0:T(8,128)(2,1)}, bf16[384,1536]{1,0:T(8,128)(2,1)}) custom-call(s32[2]{0:T(128)S(1)} %pad_add_fusion.refs_0_, bf16[256,768]{1,0:T(8,128)(2,1)} %get-tuple-element.198.refs_5_.refs_1_, f32[256,640]{1,0:T(8,128)} %get-tuple-element.195.refs_1_.refs_2_, f32[8,640]{1,0:T(8,128)S(1)} %collective-permute-done.26.refs_2_.refs_3_, ...), custom_call_target="tpu_custom_call" | custom-call | flops 603979776 | bytes 4337664 | tf_op jit(solution)/shard_map/grads/pallas_call | solution.py:700
  128.5 5.0 %collective-permute-done.28.refs_3_ = bf16[64,768]{1,0:T(8,128)(2,1)S(1)} collective-permute-done((bf16[64,768]{1,0:T(8,128)(2,1)S(1)}, bf16[64,768]{1,0:T(8,128)(2,1)S(1)}, u32[]{:S(2)}, u32[]{:S(2)}) %collective-permute-start.28) | collective-permute-done | bytes 98336 | tf_op jit(solution)/shard_map/ppermute | solution.py:716
  142.7 5.4 %collective-permute-done.31.refs_3_ = bf16[64,896]{1,0:T(8,128)(2,1)S(1)} collective-permute-done((bf16[64,896]{1,0:T(8,128)(2,1)S(1)}, bf16[64,896]{1,0:T(8,128)(2,1)S(1)}, u32[]{:S(2)}, u32[]{:S(2)}) %collective-permute-start.31) | collective-permute-done | bytes 114720 | tf_op jit(solution)/shard_map/ppermute | solution.py:716
  148.0 3.1 %gateback0.1 = (bf16[144,384]{1,0:T(8,128)(2,1)S(1)}, bf16[256,384]{1,0:T(8,128)(2,1)}, bf16[256,384]{1,0:T(8,128)(2,1)}, bf16[256,384]{1,0:T(8,128)(2,1)}, f32[8,384]{1,0:T(8,128)}, /*index=5*/bf16[256,768]{1,0:T(8,128)(2,1)}) custom-call(s32[4]{0:T(128)S(1)} %iota_xor_fusion.1.refs_0_, bf16[64,896]{1,0:T(8,128)(2,1)S(1)} %get-tuple-element.204.refs_1_, ...), custom_call_target="tpu_custom_call" | custom-call | flops 150994944 | bytes 3535872 | tf_op jit(solution)/shard_map/gateback0/pallas_call | solution.py:700
  155.6 13.7 %collective-permute-done.35.refs_2_ = bf16[144,384]{1,0:T(8,128)(2,1)S(1)} collective-permute-done((bf16[144,384]{1,0:T(8,128)(2,1)S(1)}, bf16[144,384]{1,0:T(8,128)(2,1)S(1)}, u32[]{:S(2)}, u32[]{:S(2)}) %collective-permute-start.35) | collective-permute-done | bytes 110624 | tf_op jit(solution)/shard_map/ppermute | solution.py:716
  172.2 4.6 %insideback.3 = (f32[256,384]{1,0:T(8,128)}, f32[256,256]{1,0:T(8,128)}) custom-call(bf16[256,640]{1,0:T(8,128)(2,1)} %get-tuple-element.152.refs_0_.refs_2_.refs_11_, f32[256,128]{1,0:T(8,128)} %get-tuple-element.154.refs_1_.refs_3_, f32[256,128]{1,0:T(8,128)} %get-tuple-element.153.refs_2_.refs_3_.refs_12_.refs_4_, s32[1,256]{1,0:T(1,128)} %bitcast.22, ...), custom_call_target="tpu_custom_call" | custom-call | flops 201326592 | bytes 1541120 | tf_op jit(solution)/shard_map/insideback/pallas_call | solution.py:700
  176.8 5.8 %stateback.3 = (f32[256,640]{1,0:T(8,128)}, f32[8,640]{1,0:T(8,128)S(1)}, bf16[256,128]{1,0:T(8,128)(2,1)}, f32[8,640]{1,0:T(8,128)}) custom-call(f32[128,384]{1,0:T(8,128)S(1)} %combine.23.refs_0_, bf16[128,384]{1,0:T(8,128)(2,1)} %copy-done.1, bf16[256,640]{1,0:T(8,128)(2,1)} %get-tuple-element.152.refs_0_.refs_2_.refs_11_, ...), custom_call_target="tpu_custom_call" | custom-call | flops 50331648 | bytes 3713024 | tf_op jit(solution)/shard_map/stateback/pallas_call | solution.py:700
  184.2 3.4 %backproject.3.refs_1_ = f32[256,768]{1,0:T(8,128)} custom-call(bf16[256,384]{1,0:T(8,128)(2,1)} %get-tuple-element.214.refs_0_.refs_8_, f32[256,640]{1,0:T(8,128)} %get-tuple-element.231.refs_1_.refs_2_, bf16[256,128]{1,0:T(8,128)(2,1)} %get-tuple-element.232.refs_2_.refs_4_, bf16[2,2,768,384]{3,2,1,0:T(8,128)(2,1)} %refs_3_.9, ...), custom_call_target="tpu_custom_call" | custom-call | flops 452984832 | bytes 3473408 | tf_op jit(solution)/shard_map/backproject/pallas_call | solution.py:700
  190.1 4.0 %grads.3 = (bf16[384,1536]{1,0:T(8,128)(2,1)}, bf16[384,1536]{1,0:T(8,128)(2,1)}) custom-call(s32[2]{0:T(128)S(1)} %pad_add_fusion.refs_0_, bf16[256,768]{1,0:T(8,128)(2,1)} %get-tuple-element.234.refs_5_.refs_1_, f32[256,640]{1,0:T(8,128)} %get-tuple-element.231.refs_1_.refs_2_, f32[8,640]{1,0:T(8,128)S(1)} %collective-permute-done.40.refs_2_.refs_3_, ...), custom_call_target="tpu_custom_call" | custom-call | flops 603979776 | bytes 4337664 | tf_op jit(solution)/shard_map/grads/pallas_call | solution.py:700
  208.2 4.5 %collective-permute-done.59.refs_3_ = bf16[96,384]{1,0:T(8,128)(2,1)S(1)} collective-permute-done((bf16[96,384]{1,0:T(8,128)(2,1)S(1)}, bf16[96,384]{1,0:T(8,128)(2,1)S(1)}, u32[]{:S(2)}, u32[]{:S(2)}) %collective-permute-start.59) | collective-permute-done | bytes 73760 | tf_op jit(solution)/shard_map/ppermute | solution.py:716
  218.4 4.2 %collective-permute-done.42.refs_3_ = bf16[64,768]{1,0:T(8,128)(2,1)S(1)} collective-permute-done((bf16[64,768]{1,0:T(8,128)(2,1)S(1)}, bf16[64,768]{1,0:T(8,128)(2,1)S(1)}, u32[]{:S(2)}, u32[]{:S(2)}) %collective-permute-start.42) | collective-permute-done | bytes 98336 | tf_op jit(solution)/shard_map/ppermute | solution.py:716
  237.1 3.3 %collective-permute-done.53.refs_4_ = bf16[96,384]{1,0:T(8,128)(2,1)S(1)} collective-permute-done((bf16[96,384]{1,0:T(8,128)(2,1)S(1)}, bf16[96,384]{1,0:T(8,128)(2,1)S(1)}, u32[]{:S(2)}, u32[]{:S(2)}) %collective-permute-start.53) | collective-permute-done | bytes 73760 | tf_op jit(solution)/shard_map/ppermute | solution.py:716
  245.9 3.6 %collective-permute-done.54 = bf16[96,1536]{1,0:T(8,128)(2,1)S(1)} collective-permute-done((bf16[96,1536]{1,0:T(8,128)(2,1)}, bf16[96,1536]{1,0:T(8,128)(2,1)S(1)}, u32[]{:S(2)}, u32[]{:S(2)}) %collective-permute-start.54) | collective-permute-done | bytes 294944 | tf_op jit(solution)/shard_map/ppermute | solution.py:716
  260.4 7.3 %collective-permute-done.15.refs_3_ = bf16[64,896]{1,0:T(8,128)(2,1)} collective-permute-done((bf16[64,896]{1,0:T(8,128)(2,1)}, bf16[64,896]{1,0:T(8,128)(2,1)}, u32[]{:S(2)}, u32[]{:S(2)}) %collective-permute-start.15) | collective-permute-done | bytes 114720 | tf_op jit(solution)/shard_map/ppermute | solution.py:716
  278.1 4.9 %collective-permute-done.18.refs_3_ = bf16[64,768]{1,0:T(8,128)(2,1)S(1)} collective-permute-done((bf16[64,768]{1,0:T(8,128)(2,1)S(1)}, bf16[64,768]{1,0:T(8,128)(2,1)S(1)}, u32[]{:S(2)}, u32[]{:S(2)}) %collective-permute-start.18) | collective-permute-done | bytes 98336 | tf_op jit(solution)/shard_map/ppermute | solution.py:716
  285.3 5.5 %collective-permute-done.45.refs_3_ = bf16[64,768]{1,0:T(8,128)(2,1)S(1)} collective-permute-done((bf16[64,768]{1,0:T(8,128)(2,1)}, bf16[64,768]{1,0:T(8,128)(2,1)S(1)}, u32[]{:S(2)}, u32[]{:S(2)}) %collective-permute-start.45) | collective-permute-done | bytes 98336 | tf_op jit(solution)/shard_map/ppermute | solution.py:716
  292.3 3.3 %finish1.1 = (f32[2,2,768,384]{3,2,1,0:T(8,128)}, f32[2,768,256]{2,1,0:T(8,128)}, f32[2,384,768]{2,1,0:T(8,128)}, f32[128,768]{1,0:T(8,128)}) custom-call(s32[8]{0:T(128)S(1)} %pad_add_fusion.1.refs_0_, bf16[384,1536]{1,0:T(8,128)(2,1)S(1)} %pad_maximum_fusion.1.refs_1_, bf16[384,1536]{1,0:T(8,128)(2,1)S(1)} %collective-permute-done.64.refs_2_), custom_call_target="tpu_custom_call" | custom-call | bytes 7077888 | tf_op jit(solution)/shard_map/finish1/pallas_call | solution.py:700
  295.6 4.3 %finish0.1 = (f32[2,2,768,384]{3,2,1,0:T(8,128)}, f32[2,768,256]{2,1,0:T(8,128)}, f32[2,384,768]{2,1,0:T(8,128)}, f32[128,768]{1,0:T(8,128)}, f32[2,768]{1,0:T(2...) custom-call(s32[8]{0:T(128)S(1)} %pad_add_fusion.1.refs_0_, ...), custom_call_target="tpu_custom_call", output_to_operand_aliasing={{0}: (3, {}), {1}: (4, {}), {2}: (5, {})} | custom-call | bytes 7542928 | tf_op jit(solution)/shard_map/finish0/pallas_call | solution.py:700
  (186 shorter events, 152.1 us)
Async XLA Ops:
  1.4 8.6 %collective-permute-start = (bf16[8,768]{1,0:T(8,128)(2,1)S(1)}, bf16[8,768]{1,0:T(8,128)(2,1)S(1)}, u32[]{:S(2)}, u32[]{:S(2)}) collective-permute-start(bf16[8,768]{1,0:T(8,128)(2,1)S(1)} %slice.28), channel_id=1, source_target_pairs={{0,4},{4,8},{8,12},{12,16},{16,20},{20,24},{24,28},{1,5},{5,9},{9,... | collective-permute-start | bytes 36872 | tf_op jit(solution)/shard_map/ppermute | solution.py:721
  31.8 11.0 %collective-permute-start.5 = (bf16[64,896]{1,0:T(8,128)(2,1)S(1)}, bf16[64,896]{1,0:T(8,128)(2,1)S(1)}, u32[]{:S(2)}, u32[]{:S(2)}) collective-permute-start(bf16[64,896]{1,0:T(8,128)(2,1)S(1)} %get-tuple-element.158), channel_id=1, source_target_pairs={{0,2},{1,3},{2,0},{3,1},{4,6},{5,7},{6,4},{7,5},{8,10},{9,11},{10,... | collective-permute-start | bytes 344072 | tf_op jit(solution)/shard_map/ppermute | solution.py:716
  34.4 8.4 %collective-permute-start.6 = (bf16[64,896]{1,0:T(8,128)(2,1)S(1)}, bf16[64,896]{1,0:T(8,128)(2,1)S(1)}, u32[]{:S(2)}, u32[]{:S(2)}) collective-permute-start(bf16[64,896]{1,0:T(8,128)(2,1)S(1)} %get-tuple-element.159), channel_id=1, source_target_pairs={{0,3},{1,2},{2,1},{3,0},{4,7},{5,6},{6,5},{7,4},{8,11},{9,10},{10,... | collective-permute-start | bytes 344072 | tf_op jit(solution)/shard_map/ppermute | solution.py:716
  47.2 8.6 %collective-permute-start.8 = (bf16[64,896]{1,0:T(8,128)(2,1)S(1)}, bf16[64,896]{1,0:T(8,128)(2,1)S(1)}, u32[]{:S(2)}, u32[]{:S(2)}) collective-permute-start(bf16[64,896]{1,0:T(8,128)(2,1)S(1)} %get-tuple-element.160.refs_1_), channel_id=1, source_target_pairs={{0,2},{1,3},{2,0},{3,1},{4,6},{5,7},{6,4},{7,5},{8,10},{9,11},{10,... | collective-permute-start | bytes 344072 | tf_op jit(solution)/shard_map/ppermute | solution.py:716
  121.5 18.5 %collective-permute-start.33 = (bf16[384,1536]{1,0:T(8,128)(2,1)}, bf16[384,1536]{1,0:T(8,128)(2,1)S(1)}, u32[]{:S(2)}, u32[]{:S(2)}) collective-permute-start(bf16[384,1536]{1,0:T(8,128)(2,1)} %get-tuple-element.212), channel_id=1, source_target_pairs={{0,4},{4,0},{8,12},{12,8},{16,20},{20,16},{24,28},{28,24},{1,5},{5... | collective-permute-start | bytes 3538952 | tf_op jit(solution)/shard_map/ppermute | solution.py:716
  122.7 10.8 %collective-permute-start.28 = (bf16[64,768]{1,0:T(8,128)(2,1)S(1)}, bf16[64,768]{1,0:T(8,128)(2,1)S(1)}, u32[]{:S(2)}, u32[]{:S(2)}) collective-permute-start(bf16[64,768]{1,0:T(8,128)(2,1)S(1)} %get-tuple-element.201), channel_id=1, source_target_pairs={{0,2},{1,3},{2,0},{3,1},{4,6},{5,7},{6,4},{7,5},{8,10},{9,11},{10,... | collective-permute-start | bytes 294920 | tf_op jit(solution)/shard_map/ppermute | solution.py:716
  124.9 8.6 %collective-permute-start.29 = (bf16[64,768]{1,0:T(8,128)(2,1)S(1)}, bf16[64,768]{1,0:T(8,128)(2,1)S(1)}, u32[]{:S(2)}, u32[]{:S(2)}) collective-permute-start(bf16[64,768]{1,0:T(8,128)(2,1)S(1)} %get-tuple-element.202), channel_id=1, source_target_pairs={{0,3},{1,2},{2,1},{3,0},{4,7},{5,6},{6,5},{7,4},{8,11},{9,10},{10,... | collective-permute-start | bytes 294920 | tf_op jit(solution)/shard_map/ppermute | solution.py:716
  137.4 10.7 %collective-permute-start.31 = (bf16[64,896]{1,0:T(8,128)(2,1)S(1)}, bf16[64,896]{1,0:T(8,128)(2,1)S(1)}, u32[]{:S(2)}, u32[]{:S(2)}) collective-permute-start(bf16[64,896]{1,0:T(8,128)(2,1)S(1)} %get-tuple-element.204.refs_1_), channel_id=1, source_target_pairs={{0,2},{1,3},{2,0},{3,1},{4,6},{5,7},{6,4},{7,5},{8,10},{9,11},{10,... | collective-permute-start | bytes 344072 | tf_op jit(solution)/shard_map/ppermute | solution.py:716
  137.8 10.2 %collective-permute-start.32 = (bf16[64,896]{1,0:T(8,128)(2,1)S(1)}, bf16[64,896]{1,0:T(8,128)(2,1)S(1)}, u32[]{:S(2)}, u32[]{:S(2)}) collective-permute-start(bf16[64,896]{1,0:T(8,128)(2,1)S(1)} %get-tuple-element.204.refs_1_), channel_id=1, source_target_pairs={{0,3},{1,2},{2,1},{3,0},{4,7},{5,6},{6,5},{7,4},{8,11},{9,10},{10,... | collective-permute-start | bytes 344072 | tf_op jit(solution)/shard_map/ppermute | solution.py:716
  151.2 19.2 %collective-permute-start.37 = (bf16[96,1536]{1,0:T(8,128)(2,1)S(1)}, bf16[96,1536]{1,0:T(8,128)(2,1)S(1)}, u32[]{:S(2)}, u32[]{:S(2)}) collective-permute-start(bf16[96,1536]{1,0:T(8,128)(2,1)S(1)} %copy-done.12), channel_id=1, source_target_pairs={{0,8},{4,12},{8,0},{12,4},{16,24},{20,28},{24,16},{28,20},{1,9},{5... | collective-permute-start | bytes 884744 | tf_op jit(solution)/shard_map/ppermute | solution.py:716
  152.0 18.4 %collective-permute-start.38 = (bf16[96,1536]{1,0:T(8,128)(2,1)S(1)}, bf16[96,1536]{1,0:T(8,128)(2,1)S(1)}, u32[]{:S(2)}, u32[]{:S(2)}) collective-permute-start(bf16[96,1536]{1,0:T(8,128)(2,1)S(1)} %copy-done.11), channel_id=1, source_target_pairs={{0,16},{4,20},{8,24},{12,28},{16,0},{20,4},{24,8},{28,12},{1,17},{... | collective-permute-start | bytes 884744 | tf_op jit(solution)/shard_map/ppermute | solution.py:716
  153.6 16.8 %collective-permute-start.39 = (bf16[96,1536]{1,0:T(8,128)(2,1)S(1)}, bf16[96,1536]{1,0:T(8,128)(2,1)S(1)}, u32[]{:S(2)}, u32[]{:S(2)}) collective-permute-start(bf16[96,1536]{1,0:T(8,128)(2,1)S(1)} %copy-done.10), channel_id=1, source_target_pairs={{0,24},{4,28},{8,16},{12,20},{16,8},{20,12},{24,0},{28,4},{1,25},{... | collective-permute-start | bytes 884744 | tf_op jit(solution)/shard_map/ppermute | solution.py:716
  154.8 14.5 %collective-permute-start.35 = (bf16[144,384]{1,0:T(8,128)(2,1)S(1)}, bf16[144,384]{1,0:T(8,128)(2,1)S(1)}, u32[]{:S(2)}, u32[]{:S(2)}) collective-permute-start(bf16[144,384]{1,0:T(8,128)(2,1)S(1)} %get-tuple-element.216.refs_1_), channel_id=1, source_target_pairs={{0,8},{4,12},{8,0},{12,4},{16,24},{20,28},{24,16},{28,20},{1,9},{5... | collective-permute-start | bytes 331784 | tf_op jit(solution)/shard_map/ppermute | solution.py:716
  200.6 24.5 %collective-permute-start.48 = (bf16[96,1536]{1,0:T(8,128)(2,1)}, bf16[96,1536]{1,0:T(8,128)(2,1)S(1)}, u32[]{:S(2)}, u32[]{:S(2)}) collective-permute-start(bf16[96,1536]{1,0:T(8,128)(2,1)} %get-tuple-element.248), channel_id=1, source_target_pairs={{0,8},{4,12},{8,0},{12,4},{16,24},{20,28},{24,16},{28,20},{1,9},{5... | collective-permute-start | bytes 884744 | tf_op jit(solution)/shard_map/ppermute | solution.py:716
  204.2 8.5 %collective-permute-start.59 = (bf16[96,384]{1,0:T(8,128)(2,1)S(1)}, bf16[96,384]{1,0:T(8,128)(2,1)S(1)}, u32[]{:S(2)}, u32[]{:S(2)}) collective-permute-start(bf16[96,384]{1,0:T(8,128)(2,1)S(1)} %get-tuple-element.253.refs_1_), channel_id=1, source_target_pairs={{0,2},{1,3},{2,0},{3,1},{4,6},{5,7},{6,4},{7,5},{8,10},{9,11},{10,... | collective-permute-start | bytes 221192 | tf_op jit(solution)/shard_map/ppermute | solution.py:716
  204.6 9.6 %collective-permute-start.60 = (bf16[96,384]{1,0:T(8,128)(2,1)S(1)}, bf16[96,384]{1,0:T(8,128)(2,1)S(1)}, u32[]{:S(2)}, u32[]{:S(2)}) collective-permute-start(bf16[96,384]{1,0:T(8,128)(2,1)S(1)} %get-tuple-element.253.refs_1_), channel_id=1, source_target_pairs={{0,3},{1,2},{2,1},{3,0},{4,7},{5,6},{6,5},{7,4},{8,11},{9,10},{10,... | collective-permute-start | bytes 221192 | tf_op jit(solution)/shard_map/ppermute | solution.py:716
  207.7 20.4 %collective-permute-start.49 = (bf16[96,1536]{1,0:T(8,128)(2,1)}, bf16[96,1536]{1,0:T(8,128)(2,1)S(1)}, u32[]{:S(2)}, u32[]{:S(2)}) collective-permute-start(bf16[96,1536]{1,0:T(8,128)(2,1)} %get-tuple-element.249), channel_id=1, source_target_pairs={{0,16},{4,20},{8,24},{12,28},{16,0},{20,4},{24,8},{28,12},{1,17},{... | collective-permute-start | bytes 884744 | tf_op jit(solution)/shard_map/ppermute | solution.py:716
  212.7 15.4 %collective-permute-start.50 = (bf16[96,1536]{1,0:T(8,128)(2,1)}, bf16[96,1536]{1,0:T(8,128)(2,1)S(1)}, u32[]{:S(2)}, u32[]{:S(2)}) collective-permute-start(bf16[96,1536]{1,0:T(8,128)(2,1)} %get-tuple-element.250), channel_id=1, source_target_pairs={{0,24},{4,28},{8,16},{12,20},{16,8},{20,12},{24,0},{28,4},{1,25},{... | collective-permute-start | bytes 884744 | tf_op jit(solution)/shard_map/ppermute | solution.py:716
  214.2 8.4 %collective-permute-start.42 = (bf16[64,768]{1,0:T(8,128)(2,1)S(1)}, bf16[64,768]{1,0:T(8,128)(2,1)S(1)}, u32[]{:S(2)}, u32[]{:S(2)}) collective-permute-start(bf16[64,768]{1,0:T(8,128)(2,1)S(1)} %get-tuple-element.237), channel_id=1, source_target_pairs={{0,2},{1,3},{2,0},{3,1},{4,6},{5,7},{6,4},{7,5},{8,10},{9,11},{10,... | collective-permute-start | bytes 294920 | tf_op jit(solution)/shard_map/ppermute | solution.py:716
  214.6 8.6 %collective-permute-start.43 = (bf16[64,768]{1,0:T(8,128)(2,1)S(1)}, bf16[64,768]{1,0:T(8,128)(2,1)S(1)}, u32[]{:S(2)}, u32[]{:S(2)}) collective-permute-start(bf16[64,768]{1,0:T(8,128)(2,1)S(1)} %get-tuple-element.238), channel_id=1, source_target_pairs={{0,3},{1,2},{2,1},{3,0},{4,7},{5,6},{6,5},{7,4},{8,11},{9,10},{10,... | collective-permute-start | bytes 294920 | tf_op jit(solution)/shard_map/ppermute | solution.py:716
  222.6 22.1 %collective-permute-start.61 = (bf16[96,1536]{1,0:T(8,128)(2,1)}, bf16[96,1536]{1,0:T(8,128)(2,1)S(1)}, u32[]{:S(2)}, u32[]{:S(2)}) collective-permute-start(bf16[96,1536]{1,0:T(8,128)(2,1)} %headpart.3), channel_id=1, source_target_pairs={{0,8},{4,12},{8,0},{12,4},{16,24},{20,28},{24,16},{28,20},{1,9},{5... | collective-permute-start | bytes 884744 | tf_op jit(solution)/shard_map/ppermute | solution.py:716
  223.2 22.5 %collective-permute-start.62 = (bf16[96,1536]{1,0:T(8,128)(2,1)}, bf16[96,1536]{1,0:T(8,128)(2,1)S(1)}, u32[]{:S(2)}, u32[]{:S(2)}) collective-permute-start(bf16[96,1536]{1,0:T(8,128)(2,1)} %headpart.3), channel_id=1, source_target_pairs={{0,16},{4,20},{8,24},{12,28},{16,0},{20,4},{24,8},{28,12},{1,17},{... | collective-permute-start | bytes 884744 | tf_op jit(solution)/shard_map/ppermute | solution.py:716
  225.1 20.6 %collective-permute-start.63 = (bf16[96,1536]{1,0:T(8,128)(2,1)}, bf16[96,1536]{1,0:T(8,128)(2,1)S(1)}, u32[]{:S(2)}, u32[]{:S(2)}) collective-permute-start(bf16[96,1536]{1,0:T(8,128)(2,1)} %headpart.3), channel_id=1, source_target_pairs={{0,24},{4,28},{8,16},{12,20},{16,8},{20,12},{24,0},{28,4},{1,25},{... | collective-permute-start | bytes 884744 | tf_op jit(solution)/shard_map/ppermute | solution.py:716
  242.8 9.6 %collective-permute-start.55 = (bf16[96,1536]{1,0:T(8,128)(2,1)}, bf16[96,1536]{1,0:T(8,128)(2,1)S(1)}, u32[]{:S(2)}, u32[]{:S(2)}) collective-permute-start(bf16[96,1536]{1,0:T(8,128)(2,1)} %headpart.2), channel_id=1, source_target_pairs={{0,16},{4,20},{8,24},{12,28},{16,0},{20,4},{24,8},{28,12},{1,17},{... | collective-permute-start | bytes 884744 | tf_op jit(solution)/shard_map/ppermute | solution.py:716
  244.7 9.2 %collective-permute-start.56 = (bf16[96,1536]{1,0:T(8,128)(2,1)}, bf16[96,1536]{1,0:T(8,128)(2,1)S(1)}, u32[]{:S(2)}, u32[]{:S(2)}) collective-permute-start(bf16[96,1536]{1,0:T(8,128)(2,1)} %headpart.2), channel_id=1, source_target_pairs={{0,24},{4,28},{8,16},{12,20},{16,8},{20,12},{24,0},{28,4},{1,25},{... | collective-permute-start | bytes 884744 | tf_op jit(solution)/shard_map/ppermute | solution.py:716
  245.8 46.5 %collective-permute-start.64 = (bf16[384,1536]{1,0:T(8,128)(2,1)S(1)}, bf16[384,1536]{1,0:T(8,128)(2,1)S(1)}, u32[]{:S(2)}, u32[]{:S(2)}) collective-permute-start(bf16[384,1536]{1,0:T(8,128)(2,1)S(1)} %pad_maximum_fusion.1.refs_1_), channel_id=1, source_target_pairs={{0,4},{4,0},{8,12},{12,8},{16,20},{20,16},{24,28},{28,24},{1,5},{5... | collective-permute-start | bytes 3538952 | tf_op jit(solution)/shard_map/ppermute | solution.py:716
  254.0 41.6 %collective-permute-start.57 = (bf16[384,1536]{1,0:T(8,128)(2,1)S(1)}, bf16[384,1536]{1,0:T(8,128)(2,1)}, u32[]{:S(2)}, u32[]{:S(2)}) collective-permute-start(bf16[384,1536]{1,0:T(8,128)(2,1)S(1)} %pad_maximum_fusion.refs_1_), channel_id=1, source_target_pairs={{0,4},{4,0},{8,12},{12,8},{16,20},{20,16},{24,28},{28,24},{1,5},{5... | collective-permute-start | bytes 3538952 | tf_op jit(solution)/shard_map/ppermute | solution.py:716
  255.8 11.9 %collective-permute-start.15 = (bf16[64,896]{1,0:T(8,128)(2,1)}, bf16[64,896]{1,0:T(8,128)(2,1)}, u32[]{:S(2)}, u32[]{:S(2)}) collective-permute-start(bf16[64,896]{1,0:T(8,128)(2,1)} %get-tuple-element.176), channel_id=1, source_target_pairs={{0,2},{1,3},{2,0},{3,1},{4,6},{5,7},{6,4},{7,5},{8,10},{9,11},{10,... | collective-permute-start | bytes 344072 | tf_op jit(solution)/shard_map/ppermute | solution.py:716
  256.8 10.9 %collective-permute-start.16 = (bf16[64,896]{1,0:T(8,128)(2,1)}, bf16[64,896]{1,0:T(8,128)(2,1)}, u32[]{:S(2)}, u32[]{:S(2)}) collective-permute-start(bf16[64,896]{1,0:T(8,128)(2,1)} %get-tuple-element.177), channel_id=1, source_target_pairs={{0,3},{1,2},{2,1},{3,0},{4,7},{5,6},{6,5},{7,4},{8,11},{9,10},{10,... | collective-permute-start | bytes 344072 | tf_op jit(solution)/shard_map/ppermute | solution.py:716
  272.4 10.5 %collective-permute-start.18 = (bf16[64,768]{1,0:T(8,128)(2,1)S(1)}, bf16[64,768]{1,0:T(8,128)(2,1)S(1)}, u32[]{:S(2)}, u32[]{:S(2)}) collective-permute-start(bf16[64,768]{1,0:T(8,128)(2,1)S(1)} %stream1.1.refs_1_), channel_id=1, source_target_pairs={{0,2},{1,3},{2,0},{3,1},{4,6},{5,7},{6,4},{7,5},{8,10},{9,11},{10,... | collective-permute-start | bytes 294920 | tf_op jit(solution)/shard_map/ppermute | solution.py:716
  272.4 10.5 %collective-permute-start.19 = (bf16[64,768]{1,0:T(8,128)(2,1)S(1)}, bf16[64,768]{1,0:T(8,128)(2,1)S(1)}, u32[]{:S(2)}, u32[]{:S(2)}) collective-permute-start(bf16[64,768]{1,0:T(8,128)(2,1)S(1)} %stream1.1.refs_1_), channel_id=1, source_target_pairs={{0,3},{1,2},{2,1},{3,0},{4,7},{5,6},{6,5},{7,4},{8,11},{9,10},{10,... | collective-permute-start | bytes 294920 | tf_op jit(solution)/shard_map/ppermute | solution.py:716
  275.6 9.7 %collective-permute-start.44 = (bf16[64,768]{1,0:T(8,128)(2,1)}, bf16[64,768]{1,0:T(8,128)(2,1)S(1)}, u32[]{:S(2)}, u32[]{:S(2)}) collective-permute-start(bf16[64,768]{1,0:T(8,128)(2,1)} %normback0.1.refs_1_.refs_4_), channel_id=1, source_target_pairs={{0,1},{1,0},{2,3},{3,2},{4,5},{5,4},{6,7},{7,6},{8,9},{9,8},{10,11... | collective-permute-start | bytes 294920 | tf_op jit(solution)/shard_map/ppermute | solution.py:716
  (46 other events, 308.9 us)
